TPU v7x, 1024 devices: a whole 4x8x16 slice. The times are simulated.
1024 devices in a mesh: fsdp: 16 (over z_hi, x, core), chan: 64 (over y, z_lo).
Axes of the slice: x: 4, y: 8, z: 16 (z_hi: 2, z_lo: 8; z = z_hi * 8 + z_lo), core: 2. Of those that a mesh axis runs over, the one named last changes fastest.
Arguments:
- hidden: bfloat16 [2048, 4096], P('fsdp'), may hold values from -6 to 6
- conv_out: bfloat16 [2048, 8192], P('fsdp', 'chan'), may hold values from -6 to 6
- state_in: float32 [8192, 16], P('chan'), may hold values from -6 to 6
- gate_weight: bfloat16 [4096, 8192], P('fsdp', 'chan'), may hold values from -0.09375 to 0.09375
- xproj_weight: bfloat16 [8192, 288], P('chan'), may hold values from -0.0625 to 0.0625
- dt_weight: bfloat16 [256, 8192], P(None, 'chan'), may hold values from -0.375 to 0.375
- dt_bias: float32 [8192], P('chan'), may hold values from -7 to -1
- a_log: float32 [8192, 16], P('chan'), may hold values from -1.5 to 2.77
- skip_gain: float32 [8192], P('chan'), may hold values from 0.25 to 1
- out_weight: bfloat16 [4096, 8192], P('fsdp', 'chan'), may hold values from -0.0625 to 0.0625
Outputs:
- mixed: bfloat16 [2048, 4096], P(('fsdp', 'chan'))
All inputs are finite; a program needn't handle non-finite values.
Results may differ from a plain program's by a relative error of at most 0.007.
Values may be sent and summed in bfloat16 or wider, within the bound.
No kernel may reach another device: no remote copies, remote signals or barrier semaphores. Data moves between devices by JAX's collectives and lax.ppermute only.
A program may use at most 32 MiB of HBM per device.

v0:
```python
import functools

import jax
import jax.numpy as jnp
from jax import lax
from jax.sharding import Mesh
from jax.sharding import PartitionSpec as P

STATE = 16
RANK = 256
BLOCK = 16
CHAN = ("chan_0", "chan_1")
FSDP_CHAN = ("fsdp", "chan_0", "chan_1")


def one_axis_at_a_time(array, axes):
    return functools.reduce(lax.psum, axes, array)


def sent_together(arrays, axis, dim, along):
    columns = [a.reshape(*a.shape[:along], -1) for a in arrays]
    both = jnp.concatenate(columns, axis=along)
    filled, at, outs = (lax.all_gather(both, axis, axis=dim, tiled=True), 0, [])
    for a, column in zip(arrays, columns):
        piece = filled[..., at : at + column.shape[along]]
        outs.append(piece.reshape(*piece.shape[:along], *a.shape[along:]))
        at += column.shape[along]
    return tuple(outs)


def sent_together_2(arrays, axis, dim, along):
    both = jnp.concatenate(arrays, axis=along)
    filled, at, outs = (lax.all_gather(both, axis, axis=dim, tiled=True), 0, [])
    for a in arrays:
        outs.append(lax.slice_in_dim(filled, at, at + a.shape[along], axis=along))
        at += a.shape[along]
    return tuple(outs)


def sum_by_axis(so_far, axes):
    for axis in axes:
        so_far = lax.psum_scatter(so_far, axis, scatter_dimension=0, tiled=True)
    return so_far


def shards(
    hidden,
    conv_out,
    state_in,
    gate_weight,
    xproj_weight,
    dt_weight,
    dt_bias,
    a_log,
    skip_gain,
    out_weight,
):
    rows_here, channels = conv_out.shape
    partial_value = jnp.dot(conv_out, xproj_weight, preferred_element_type=jnp.float32)
    projected = one_axis_at_a_time(partial_value, CHAN)
    step_low = projected[:, :RANK].astype(jnp.bfloat16)
    in_coef = projected[:, RANK : RANK + STATE]
    out_coef = projected[:, RANK + STATE :]
    step_size = jax.nn.softplus(
        jnp.dot(step_low, dt_weight, preferred_element_type=jnp.float32) + dt_bias
    )
    decay_rate = -jnp.exp(a_log)
    inputs = conv_out.astype(jnp.float32)
    blocks = rows_here // BLOCK
    position_rows = lax.broadcasted_iota(jnp.int32, (BLOCK, BLOCK), 0)
    position_cols = lax.broadcasted_iota(jnp.int32, (BLOCK, BLOCK), 1)
    causal_mask = position_rows >= position_cols

    def block_step(carry_state, block_items):
        step_blk, input_blk, in_blk, out_blk = block_items
        within = jnp.cumsum(step_blk, axis=0)
        spread = jnp.where(causal_mask[:, :, None], within[:, None, :] - within[None, :, :], 0.0)
        weights = jnp.where(
            causal_mask[:, :, None, None], jnp.exp(spread[:, :, :, None] * decay_rate), 0.0
        )
        driven = (step_blk * input_blk)[:, :, None] * in_blk[:, None, :]
        states = jnp.einsum("tscn,scn->tcn", weights, driven, precision=lax.Precision.HIGHEST)
        states = states + jnp.exp(within[:, :, None] * decay_rate) * carry_state[None]
        block_out = jnp.einsum("tcn,tn->tc", states, out_blk, precision=lax.Precision.HIGHEST)
        return (states[-1], block_out)

    def split_blocks(values):
        return values.reshape((blocks, BLOCK) + values.shape[1:])

    empty_state = jnp.zeros((channels, STATE), jnp.float32)
    last_state, local_out = lax.scan(
        block_step,
        empty_state,
        (
            split_blocks(step_size),
            split_blocks(inputs),
            split_blocks(in_coef),
            split_blocks(out_coef),
        ),
    )
    local_out = local_out.reshape((rows_here, channels))
    total_step = jnp.sum(step_size, axis=0)
    totals, finals = sent_together((total_step[None], last_state[None]), "fsdp", 0, 2)
    position = lax.axis_index("fsdp")
    sources = jnp.arange(totals.shape[0], dtype=jnp.int32)
    earlier_mask = sources < position
    through_sum = jnp.cumsum(totals, axis=0)
    before_sum = jnp.sum(jnp.where(earlier_mask[:, None], totals, 0.0), axis=0)
    gap_steps = jnp.where(earlier_mask[:, None], before_sum[None, :] - through_sum, 0.0)
    factor = jnp.where(
        earlier_mask[:, None, None], jnp.exp(gap_steps[:, :, None] * decay_rate), 0.0
    )
    entering = (
        jnp.sum(factor * finals, axis=0) + jnp.exp(before_sum[:, None] * decay_rate) * state_in
    )
    through = jnp.cumsum(step_size, axis=0)
    carried = jnp.einsum(
        "tcn,tn->tc",
        jnp.exp(through[:, :, None] * decay_rate) * entering[None],
        out_coef,
        precision=lax.Precision.HIGHEST,
    )
    scanned = local_out + carried
    gate_full, out_full = sent_together_2((gate_weight, out_weight), "fsdp", 0, 1)
    gate_pre = jnp.dot(hidden, gate_full, preferred_element_type=jnp.float32)
    gated_out = ((scanned + skip_gain * inputs) * jax.nn.silu(gate_pre)).astype(jnp.bfloat16)
    summed = sum_by_axis(
        lax.dot_general(
            gated_out, out_full, (((1,), (1,)), ((), ())), preferred_element_type=jnp.float32
        ),
        CHAN,
    )
    mixed = summed.astype(jnp.bfloat16)
    return mixed


def solution(mesh):
    torus = Mesh(mesh.devices.reshape(mesh.shape["fsdp"], 8, 8), ("fsdp", "chan_0", "chan_1"))
    return jax.shard_map(
        shards,
        mesh=torus,
        in_specs=(
            P("fsdp", None),
            P("fsdp", CHAN),
            P(CHAN, None),
            P("fsdp", CHAN),
            P(CHAN, None),
            P(None, CHAN),
            P(CHAN),
            P(CHAN, None),
            P(CHAN),
            P("fsdp", CHAN),
        ),
        out_specs=P(FSDP_CHAN, None),
        check_vma=False,
    )
```

profile of v0, /device:TPU:6, one launch (start us, length us, event | category | flops | bytes accessed | tf_op | source)
XLA Modules:
  0.0 443.4 jit_solution(11332771418636830052)
XLA Ops:
  7.4 1.8 fusion.20
  9.3 97.8 %all-reduce.5.cloned.1.call-done = f32[128,288]{0,1:T(8,128)} async-done(((f32[128,288]{0,1:T(8,128)}), f32[128,288]{0,1:T(8,128)}) %all-reduce.5.cloned.1.call-update) | async-done | bytes 147472 | tf_op jit(solution)/shard_map/psum | solution.py:17
  107.1 1.5 pad_maximum_fusion
  108.7 0.9 copy.55
  109.6 0.7 exponential_negate_fusion
  110.4 137.6 %all-reduce.7.cloned.1.call-done = f32[128,288]{0,1:T(8,128)} async-done(((f32[128,288]{0,1:T(8,128)}), f32[128,288]{0,1:T(8,128)}) %all-reduce.7.cloned.1.call-update) | async-done | bytes 147472 | tf_op jit(solution)/shard_map/psum | solution.py:17
  248.1 0.7 fusion.17
  249.0 1.2 fusion.18
  250.2 32.2 %while.14 = (s32[]{:T(128)}, f32[128,16]{1,0:T(8,128)S(1)}, f32[8,16,128]{2,1,0:T(8,128)S(1)}, f32[8,16,128]{2,1,0:T(8,128)S(1)}, f32[8,16,128]{2,1,0:T(8,128)S(...) while((s32[]{:T(128)}, f32[128,16]{1,0:T(8,128)S(1)}, ...), condition=%wide.region_4.5_spmd.clone.clone, body=%wide.region_2.4_spmd.clone.clone.sunk | while | flops 2687234 | bytes 1743741 | solution.py:91
  251.1 0.6 multiply_reduce_fusion.3
  252.5 1.7 fusion.32
  255.1 0.6 multiply_reduce_fusion.3
  256.5 1.7 fusion.32
  259.1 0.6 multiply_reduce_fusion.3
  260.5 1.7 fusion.32
  263.1 0.6 multiply_reduce_fusion.3
  264.5 1.7 fusion.32
  267.2 0.6 multiply_reduce_fusion.3
  268.6 1.7 fusion.32
  271.2 0.6 multiply_reduce_fusion.3
  272.6 1.7 fusion.32
  275.2 0.6 multiply_reduce_fusion.3
  276.6 1.7 fusion.32
  279.2 0.6 multiply_reduce_fusion.3
  280.6 1.7 fusion.32
  282.6 33.2 %all_gather.6 = f32[16,128,17]{1,2,0:T(8,128)S(1)} all-gather(f32[1,128,17]{1,2,0:T(8,128)S(1)} %pad_maximum_fusion.1), channel_id=1, replica_groups=mesh['fsdp'=16,'chan_0'=8,'chan_1'=8] {'fsdp'}, dimensions={0}, use_global_device_ids=true | all-gather | bytes 147968 | tf_op jit(solution)/shard_map/all_gather | solution.py:23
  316.2 0.4 multiply_reduce_fusion.1
  316.9 4.3 fusion.2
  321.2 1.3 dynamic-slice
  323.1 49.4 %reduce-scatter.2.cloned.1.call-done = f32[16,4096]{1,0:T(8,128)} async-done(((f32[128,4096]{1,0:T(8,128)}), f32[16,4096]{1,0:T(8,128)}) %reduce-scatter.2.cloned.1.call-update) | async-done | bytes 262160 | tf_op jit(solution)/shard_map/reduce_scatter | solution.py:42
  372.5 63.1 %all-reduce.8 = bf16[16,4096]{1,0:T(8,128)(2,1)S(1)} all-reduce(f32[16,4096]{1,0:T(8,128)} %reduce-scatter.2.cloned.1.call-done), channel_id=3, replica_groups=mesh['fsdp'=16,'chan_0'=8,'chan_1'=8] {'chan_1'}, use_global_device_ids=true, to_apply=%region_11.12.clone | all-reduce | flops 65536 | bytes 393216
  435.6 0.6 dynamic-slice_convert_fusion
  (146 shorter events, 14.2 us)
Async XLA Ops:
  7.4 309.5 %copy-start = (bf16[128,4096]{1,0:T(8,128)(2,1)S(1)}, bf16[128,4096]{1,0:T(8,128)(2,1)}, u32[]{:S(2)}) copy-start(bf16[128,4096]{1,0:T(8,128)(2,1)} %param.12) | copy-start | bytes 3145732
  7.4 99.7 %all-reduce.5.cloned.1.call-start = ((), (), s32[]{:S(2)}) async-start(), calls=%async_computation.1 | async-start | bytes 294912 | tf_op jit(solution)/shard_map/psum | solution.py:17
  9.2 238.8 %all-reduce.7.cloned.1.call-start = ((), (), s32[]{:S(2)}) async-start(), calls=%async_computation.2 | async-start | bytes 294912 | tf_op jit(solution)/shard_map/psum | solution.py:17
  107.1 209.8 %all-gather.2.cloned.1.call-start = ((), (), s32[]{:S(2)}) async-start(), calls=%async_computation.3 | async-start | bytes 2228224 | tf_op jit(solution)/shard_map/all_gather | solution.py:33
  108.7 263.8 %reduce-scatter.2.cloned.1.call-start = ((), (), s32[]{:S(2)}) async-start(), calls=%async_computation.4 | async-start | bytes 2359296 | tf_op jit(solution)/shard_map/reduce_scatter | solution.py:42
  250.2 66.0 %copy-start.1 = (f32[128,16]{0,1:T(8,128)S(1)}, f32[128,16]{0,1:T(8,128)}, u32[]{:S(2)}) copy-start(f32[128,16]{0,1:T(8,128)} %param.19) | copy-start | bytes 24580
  250.2 66.0 %copy-start.2 = (f32[128,16]{0,1:T(8,128)S(1)}, f32[128,16]{0,1:T(8,128)}, u32[]{:S(2)}) copy-start(f32[128,16]{0,1:T(8,128)} %param.14) | copy-start | bytes 24580
  250.2 66.7 %copy-start.3 = (f32[128]{0:T(128)S(1)}, f32[128]{0:T(128)}, u32[]{:S(2)}) copy-start(f32[128]{0:T(128)} %param.20) | copy-start | bytes 1540
Sparse Core Ops, SparseCore 0:
  10.5 96.4 all-reduce.4
  110.5 137.4 all-reduce.6
  321.3 51.1 reduce-scatter.1
Sparse Core Ops, SparseCore 1:
  112.0 97.2 all-gather.1
where the time goes:
time: 444 us; the launch traced here: 443 us
  waiting for transfers between devices  285 us (64%)
  blocking collectives  96.4 us (22%)
  matrix products  21.1 us (5%)
  between operations  15.4 us (3%)
  other arithmetic  14.6 us (3%)
  local copies, waits for them, and re-layouts  10.2 us (2%)
    psum x2, waiting for transfers between devices, one_axis_at_a_time(): return functools.reduce(lax.psum, axes, array)  235 us
    unnamed x1, blocking collectives  63.1 us
    reduce_scatter x1, waiting for transfers between devices, sum_by_axis(): so_far = lax.psum_scatter(so_far, axis, scatter_dimension=0, tiled=True)  49.4 us
    all_gather x1, blocking collectives, sent_together(): filled, at, outs = (lax.all_gather(both, axis, axis=dim, tiled=True), 0, [])  33.2 us
    dot_general x8, matrix products, block_step(): jnp.einsum('tcn,tn->tc', states, out_blk, precision=lax.Precision.HIGHEST)  13.8 us
  transfers between devices with their start and end apart: 4, of which 3 were waited for; matrix products, arithmetic and copies ran while one was open for 9% of the time, Pallas kernels for 0%

commit v1 on v0

v1 whole, which is shorter than its diff:
```python
import jax
import jax.numpy as jnp
from jax import lax
from jax.experimental import pallas as pl
from jax.experimental.pallas import tpu as pltpu
from jax.sharding import Mesh
from jax.sharding import PartitionSpec as P

STATE = 16
RANK = 256
FSDP = ("zh", "x", "core")
CHAN = ("y", "z")
FSDP_CHAN = FSDP + CHAN
SPLIT = {16: (2, 4, 2), 64: (8, 8)}
PAYLOAD = 24
LOG2E = 1.4426950408889634
VMEM = pl.BlockSpec(memory_space=pltpu.VMEM)
SMEM = pl.BlockSpec(memory_space=pltpu.SMEM)


def exchange(array, axes):
    return lax.all_to_all(array, axes, 0, 0, tiled=True)


def near_core(array):
    return pltpu.with_memory_space_constraint(array, pltpu.VMEM)


def project_kernel(xproj, conv, out):
    pieces, piece, rows = out.shape
    share = lax.dot_general(
        xproj[...], conv[...], (((1,), (1,)), ((), ())), preferred_element_type=jnp.float32
    )
    share = jnp.concatenate([share, share[RANK:]], axis=0).astype(out.dtype)
    used = share.shape[0] // piece
    out[:used] = share.reshape(used, piece, rows)
    if used < pieces:
        out[used:] = jnp.zeros((pieces - used, piece, rows), out.dtype)


def add_kernel(at, shares, out):
    _, piece, _ = shares.shape
    total = jnp.sum(shares[...].astype(jnp.float32), axis=0)
    high = total.astype(jnp.bfloat16).astype(jnp.float32)
    row = at[0] * piece + lax.broadcasted_iota(jnp.int32, total.shape, 0)
    chosen = jnp.where(row >= RANK + 2 * STATE, total - high, high).astype(jnp.bfloat16)
    out[...] = jnp.broadcast_to(chosen[None], out.shape)


def coefficients(proj, first, count):
    low = first + 2 * STATE
    return proj[first : first + count].astype(jnp.float32) + proj[low : low + count].astype(
        jnp.float32
    )


def step_sizes(low, dt_weight, dt_bias):
    v = lax.dot_general(
        low, dt_weight, (((0,), (0,)), ((), ())), preferred_element_type=jnp.float32
    )
    v = v + dt_bias
    return jnp.maximum(v, 0.0) + jnp.log1p(jnp.exp(-jnp.abs(v)))


def local_kernel(proj, conv, dt_weight, dt_bias, a_log, step_out, pay_out):
    rows = conv.shape[0]
    step = step_sizes(proj[:RANK], dt_weight[...], dt_bias[...])
    step_out[...] = step
    rate = -jnp.exp(a_log[...]) * LOG2E
    driven = step * conv[...].astype(jnp.float32)
    coef = coefficients(proj, RANK, STATE)
    state = jnp.zeros((STATE, step.shape[1]), jnp.float32)
    for t in range(rows):
        state = jnp.exp2(step[t : t + 1] * rate) * state + driven[t : t + 1] * coef[:, t : t + 1]
    total = jnp.sum(step, axis=0, keepdims=True)
    high = total.astype(jnp.bfloat16).astype(jnp.float32)
    rest = jnp.zeros((PAYLOAD - STATE - 2, step.shape[1]), jnp.float32)
    payload = jnp.concatenate([state, high, total - high, rest], axis=0).astype(jnp.bfloat16)
    pay_out[...] = jnp.broadcast_to(payload[None], pay_out.shape)


def gate_kernel(here, hidden, kept, swapped, out):
    n_x, depth, _ = kept.shape
    block = depth // 4
    total = jnp.zeros(out.shape, jnp.float32)
    for other, weight in enumerate((kept, swapped)):
        for back in range(n_x):
            for turn in range(2):
                line = (here[0] + turn) % 2 * n_x + (here[1] + n_x - back) % n_x
                at = (line * 2 + (here[2] + other) % 2) * block
                total += jnp.dot(
                    hidden[:, pl.ds(pl.multiple_of(at, block), block)],
                    weight[back, turn * block : (turn + 1) * block],
                    preferred_element_type=jnp.float32,
                )
    out[...] = total


def scan_kernel(step_in, proj, conv, a_log, skip, out, through):
    rows = conv.shape[0]
    rate = -jnp.exp(a_log[...]) * LOG2E
    step = step_in[...]
    inputs = conv[...].astype(jnp.float32)
    driven = step * inputs
    direct = skip[...] * inputs
    coefs = coefficients(proj, RANK, 2 * STATE)
    state = jnp.zeros((STATE, step.shape[1]), jnp.float32)
    summed = jnp.zeros((1, step.shape[1]), jnp.float32)
    for t in range(rows):
        now = step[t : t + 1]
        summed = summed + now
        through[t : t + 1] = summed
        state = jnp.exp2(now * rate) * state + driven[t : t + 1] * coefs[:STATE, t : t + 1]
        value = jnp.sum(state * coefs[STATE:, t : t + 1], axis=0, keepdims=True)
        out[t : t + 1] = value + direct[t : t + 1]


def gated_kernel(pos, through, local, proj, a_log, state_in, gathered, gate_pre, out, carried):
    rows = local.shape[0]
    rate = -jnp.exp(a_log[...]) * LOG2E
    state = state_in[...]
    for source in range(gathered.shape[0]):
        payload = gathered[source].astype(jnp.float32)
        total = payload[STATE : STATE + 1] + payload[STATE + 1 : STATE + 2]
        moved = jnp.exp2(total * rate) * state + payload[:STATE]
        state = jnp.where(source < pos[0], moved, state)
    coefs = coefficients(proj, RANK + STATE, STATE)
    for t in range(rows):
        left = jnp.exp2(through[t : t + 1] * rate) * state
        carried[t : t + 1] = jnp.sum(left * coefs[:, t : t + 1], axis=0, keepdims=True)
    gate = gate_pre[...]
    value = (carried[...] + local[...]) * (gate / (1.0 + jnp.exp(-gate)))
    out[...] = jnp.broadcast_to(value.astype(jnp.bfloat16)[None], out.shape)


def mix_kernel(here, gated, kept, swapped, out, total, staged):
    n_x, depth, _ = kept.shape
    block = depth // 4
    tiles, rows, lanes = total.shape
    pieces, height, _ = out.shape
    own = rows // pieces
    per = block // lanes
    for other, weight in enumerate((kept, swapped)):
        part = jnp.zeros((rows, block), jnp.float32)
        for back in range(n_x):
            for turn in range(2):
                line = (here[0] + turn) % 2 * n_x + (here[1] + n_x - back) % n_x
                part += lax.dot_general(
                    gated[line],
                    weight[back, (2 + turn) * block : (3 + turn) * block],
                    (((1,), (1,)), ((), ())),
                    preferred_element_type=jnp.float32,
                )
        for k in range(per):
            total[(here[2] + other) % 2 * per + k] = part[:, k * lanes : (k + 1) * lanes]
    for row in range(own):
        for tile in range(tiles):
            staged[pl.ds(row * tiles + tile, pieces, stride=height), :] = total[
                tile, pl.ds(row, pieces, stride=own), :
            ]
    out[...] = staged[...].astype(jnp.bfloat16).reshape(out.shape)


def last_kernel(shares, out, rows):
    own, width = out.shape
    pieces, height, lanes = shares.shape
    tiles = height // own
    lines = width // (tiles * lanes)
    total = shares[...].astype(jnp.float32).reshape(lines, pieces // lines, height, lanes)
    total = jnp.sum(total, axis=1)
    for line in range(lines):
        for row in range(own):
            for tile in range(tiles):
                at = (line * tiles + tile) * lanes
                rows[row : row + 1, at : at + lanes] = total[
                    line, row * tiles + tile : row * tiles + tile + 1
                ]
    out[...] = rows[...].astype(jnp.bfloat16)


def shards_for(sizes):
    n_zh, n_x, n_core, n_y, n_z = sizes
    n_f, n_c = n_zh * n_x * n_core, n_y * n_z

    def turned(flip):
        pairs = []
        for zh in range(n_zh):
            for x in range(n_x):
                for core in range(n_core):
                    for y in range(n_y):
                        source = ((zh * n_x + x) * n_core + core) * n_y + y
                        to_zh, to_x = (y // n_x + flip) % n_zh, y % n_x
                        target = ((to_zh * n_x + to_x) * n_core + core) * n_y + zh * n_x + x
                        pairs.append((source, target))
        return pairs

    def shards(
        hidden, conv_out, state_in, gate_weight, xproj_weight, dt_weight, dt_bias, a_log, skip_gain, out_weight
    ):
        rows, channels = conv_out.shape
        own = rows // n_c
        here = jnp.stack([lax.axis_index(axis) for axis in FSDP]).astype(jnp.int32)
        own_piece = lax.axis_index(CHAN).astype(jnp.int32)[None]
        position = lax.axis_index(FSDP).astype(jnp.int32)[None]
        bf16, f32 = jnp.bfloat16, jnp.float32
        shape = jax.ShapeDtypeStruct

        gate_far = lax.ppermute(gate_weight, "zh", [(0, 1), (1, 0)])
        out_near = lax.ppermute(out_weight, FSDP + ("y",), turned(0))
        out_far = lax.ppermute(out_weight, FSDP + ("y",), turned(1))

        used = xproj_weight.shape[1] + 2 * STATE
        piece = -(-used // (8 * n_c)) * 8
        shares = pl.pallas_call(project_kernel, out_shape=shape((n_c, piece, rows), bf16))(
            xproj_weight.T, conv_out
        )
        shares = exchange(shares, CHAN)
        summed = pl.pallas_call(
            add_kernel, in_specs=[SMEM, VMEM], out_shape=shape(shares.shape, bf16)
        )(own_piece, near_core(shares))
        proj = exchange(summed, CHAN).reshape(n_c * piece, rows)

        mine = jnp.concatenate([gate_weight, gate_far, out_near, out_far], axis=0)
        kept = [mine]
        for back in range(1, n_x):
            kept.append(lax.ppermute(mine, "x", [(i, (i + back) % n_x) for i in range(n_x)]))
        kept = jnp.stack(kept)
        swapped = near_core(lax.ppermute(kept, "core", [(0, 1), (1, 0)]))
        kept = near_core(kept)

        proj, log_rate = near_core(proj), a_log.T
        step, payload = pl.pallas_call(
            local_kernel,
            out_shape=(shape((rows, channels), f32), shape((n_f, PAYLOAD, channels), bf16)),
        )(proj, conv_out, dt_weight, dt_bias[None], log_rate)
        gathered = near_core(exchange(payload, FSDP))
        local, through = pl.pallas_call(
            scan_kernel, out_shape=(shape((rows, channels), f32),) * 2
        )(step, proj, conv_out, log_rate, skip_gain[None])
        gate_pre = pl.pallas_call(
            gate_kernel, in_specs=[SMEM] + [VMEM] * 3, out_shape=shape((rows, channels), f32)
        )(here, hidden, kept, swapped)
        gated = pl.pallas_call(
            gated_kernel,
            in_specs=[SMEM] + [VMEM] * 7,
            out_shape=shape((n_y, rows, channels), bf16),
            scratch_shapes=[pltpu.VMEM((rows, channels), f32)],
        )(position, through, local, proj, log_rate, state_in.T, gathered, gate_pre)
        line = near_core(exchange(gated, "y"))

        width = hidden.shape[1] // n_y
        lanes = min(128, width // n_core)
        tiles = width // lanes
        sums = pl.pallas_call(
            mix_kernel,
            in_specs=[SMEM] + [VMEM] * 3,
            out_shape=shape((n_c, own * tiles, lanes), bf16),
            scratch_shapes=[
                pltpu.VMEM((tiles, rows, lanes), f32),
                pltpu.VMEM((rows * tiles, lanes), f32),
            ],
        )(here, line, kept, swapped)
        sums = near_core(exchange(sums, CHAN))
        return pl.pallas_call(
            last_kernel,
            out_shape=jax.ShapeDtypeStruct((own, n_y * width), bf16),
            scratch_shapes=[pltpu.VMEM((own, n_y * width), f32)],
        )(sums)

    return shards


def solution(mesh):
    sizes = SPLIT[mesh.shape["fsdp"]] + SPLIT[mesh.shape["chan"]]
    torus = Mesh(mesh.devices.reshape(sizes), FSDP_CHAN)
    return jax.shard_map(
        shards_for(sizes),
        mesh=torus,
        in_specs=(
            P(FSDP, None),
            P(FSDP, CHAN),
            P(CHAN, None),
            P(FSDP, CHAN),
            P(CHAN, None),
            P(None, CHAN),
            P(CHAN),
            P(CHAN, None),
            P(CHAN),
            P(FSDP, CHAN),
        ),
        out_specs=P(FSDP_CHAN, None),
        check_vma=False,
    )
```

time: 444 us -> 176 us (0.40)
  waiting for transfers between devices: 285 us -> 35.1 us
  starting transfers between devices: 0.13 us -> 65 us
  blocking collectives: 96.4 us -> 58.4 us
  matrix products: 21.1 us -> 0 us
  between operations: 15.4 us -> 0.14 us
  Pallas kernels: 0 us -> 14.2 us
  other arithmetic: 14.6 us -> 0.69 us
  local copies, waits for them, and re-layouts: 10.2 us -> 0.9 us
    psum x2 -> x0, waiting for transfers between devices: 235 us -> none  [one_axis_at_a_time(): return functools.reduce(lax.psum, axes, array)]
    unnamed x1 -> x0, blocking collectives: 63.1 us -> none
    all_to_all x0 -> x3, blocking collectives: none -> 58.4 us  [exchange(): return lax.all_to_all(array, axes, 0, 0, tiled=True)]
    reduce_scatter x1 -> x0, waiting for transfers between devices: 49.4 us -> none  [sum_by_axis(): so_far = lax.psum_scatter(so_far, axis, scatter_dimension=0, tiled=True)]
    ppermute x0 -> x7, starting transfers between devices: none -> 39.4 us  [the longest x1 22.3 us: shards(): out_far = lax.ppermute(out_weight, FSDP + ('y',), turned(1))]
    all_gather x1 -> x0, blocking collectives: 33.2 us -> none  [sent_together(): filled, at, outs = (lax.all_gather(both, axis, axis=dim, tiled=True), 0, [])]
    all_to_all x0 -> x2, starting transfers between devices: none -> 25.5 us  [exchange(): return lax.all_to_all(array, axes, 0, 0, tiled=True)]
    dot_general x11 -> x0, matrix products: 21.1 us -> none  [the longest x8 13.8 us: block_step(): jnp.einsum('tcn,tn->tc', states, out_blk, precision=lax.Precision.HIGHEST)]
  transfers between devices with their start and end apart: 4 -> 9, of which waited for: 3 -> 3; matrix products, arithmetic and copies ran while one was open for 9% -> 1% of each run, Pallas kernels for 0% -> 5%
where the time goes in v1:
time: 176 us; the launch traced here: 175 us
  starting transfers between devices  65 us (37%)
  blocking collectives  58.4 us (33%)
  waiting for transfers between devices  35.1 us (20%)
  Pallas kernels  14.2 us (8%)
    all_to_all x3, blocking collectives, exchange(): return lax.all_to_all(array, axes, 0, 0, tiled=True)  58.4 us
    all_to_all x2, starting transfers between devices, exchange(): return lax.all_to_all(array, axes, 0, 0, tiled=True)  25.5 us
    ppermute x1, starting transfers between devices, shards(): out_far = lax.ppermute(out_weight, FSDP + ('y',), turned(1))  22.3 us
    all_to_all x2, waiting for transfers between devices, exchange(): return lax.all_to_all(array, axes, 0, 0, tiled=True)  20.5 us
    ppermute x1, waiting for transfers between devices, shards(): gate_far = lax.ppermute(gate_weight, 'zh', [(0, 1), (1, 0)])  14.6 us
    ppermute x3, starting transfers between devices, shards(): lax.ppermute(mine, 'x', [(i, (i + back) % n_x) for i in range(n_x)])  8.97 us
    ppermute x1, starting transfers between devices, shards(): out_near = lax.ppermute(out_weight, FSDP + ('y',), turned(0))  4.33 us
  transfers between devices with their start and end apart: 9, of which 3 were waited for; matrix products, arithmetic and copies ran while one was open for 1% of the time, Pallas kernels for 5%

profile of v1, /device:TPU:6, one launch (start us, length us, event | category | flops | bytes accessed | tf_op | source)
XLA Modules:
  0.0 174.5 jit_solution(7369659330246607706)
XLA Ops:
  0.0 22.3 %collective-permute-start.2 = (bf16[256,128]{1,0:T(8,128)(2,1)}, bf16[256,128]{1,0:T(8,128)(2,1)S(1)}, u32[]{:S(2)}, u32[]{:S(2)}) collective-permute-start(bf16[256,128]{1,0:T(8,128)(2,1)} %param.19), channel_id=1, source_target_pairs={{0,512},{8,640},{16,768},{24,896},{32,0},{40,128},{48,256},{56,384... | collective-permute-start | bytes 196616 | tf_op jit(solution)/shard_map/ppermute | solution.py:210
  22.3 4.3 %collective-permute-start.1 = (bf16[256,128]{1,0:T(8,128)(2,1)}, bf16[256,128]{1,0:T(8,128)(2,1)S(1)}, u32[]{:S(2)}, u32[]{:S(2)}) collective-permute-start(bf16[256,128]{1,0:T(8,128)(2,1)} %param.19), channel_id=1, source_target_pairs={{0,0},{8,128},{16,256},{24,384},{32,512},{40,640},{48,768},{56,896... | collective-permute-start | bytes 196616 | tf_op jit(solution)/shard_map/ppermute | solution.py:209
  26.6 1.9 %collective-permute-start = (bf16[256,128]{1,0:T(8,128)(2,1)}, bf16[256,128]{1,0:T(8,128)(2,1)S(1)}, u32[]{:S(2)}, u32[]{:S(2)}) collective-permute-start(bf16[256,128]{1,0:T(8,128)(2,1)} %param.13), channel_id=1, source_target_pairs={{0,512},{512,0},{1,513},{513,1},{2,514},{514,2},{3,515},{515,3},{4... | collective-permute-start | bytes 196616 | tf_op jit(solution)/shard_map/ppermute | solution.py:208
  28.6 0.9 constant_dynamic-update-slice_fusion.3
  29.4 14.6 %collective-permute-done = bf16[256,128]{1,0:T(8,128)(2,1)S(1)} collective-permute-done((bf16[256,128]{1,0:T(8,128)(2,1)}, bf16[256,128]{1,0:T(8,128)(2,1)S(1)}, u32[]{:S(2)}, u32[]{:S(2)}) %collective-permute-start) | collective-permute-done | bytes 65568 | tf_op jit(solution)/shard_map/ppermute | solution.py:208
  44.0 0.0 collective-permute-done.1
  44.0 0.0 collective-permute-done.2
  44.1 1.9 %collective-permute-start.5 = (bf16[1024,128]{1,0:T(8,128)(2,1)S(1)}, bf16[1024,128]{1,0:T(8,128)(2,1)S(1)}, u32[]{:S(2)}, u32[]{:S(2)}) collective-permute-start(bf16[1024,128]{1,0:T(8,128)(2,1)S(1)} %constant_dynamic-update-slice_fusion), channel_id=1, source_target_pairs={{0,384},{128,0},{256,128},{384,256},{1,385},{129,1},{257,129},{385... | collective-permute-start | bytes 786440 | tf_op jit(solution)/shard_map/ppermute | solution.py:226
  46.0 1.9 %collective-permute-start.4 = (bf16[1024,128]{1,0:T(8,128)(2,1)S(1)}, bf16[1024,128]{1,0:T(8,128)(2,1)S(1)}, u32[]{:S(2)}, u32[]{:S(2)}) collective-permute-start(bf16[1024,128]{1,0:T(8,128)(2,1)S(1)} %constant_dynamic-update-slice_fusion), channel_id=1, source_target_pairs={{0,256},{128,384},{256,0},{384,128},{1,257},{129,385},{257,1},{385... | collective-permute-start | bytes 786440 | tf_op jit(solution)/shard_map/ppermute | solution.py:226
  47.9 5.1 %collective-permute-start.3 = (bf16[1024,128]{1,0:T(8,128)(2,1)S(1)}, bf16[1024,128]{1,0:T(8,128)(2,1)S(1)}, u32[]{:S(2)}, u32[]{:S(2)}) collective-permute-start(bf16[1024,128]{1,0:T(8,128)(2,1)S(1)} %constant_dynamic-update-slice_fusion), channel_id=1, source_target_pairs={{0,128},{128,256},{256,384},{384,0},{1,129},{129,257},{257,385},{3... | collective-permute-start | bytes 786440 | tf_op jit(solution)/shard_map/ppermute | solution.py:226
  53.1 1.7 shard_map.100
  54.8 15.3 %all-to-all-start = ((bf16[64,8,128]{2,1,0:T(8,128)(2,1)}), bf16[64,8,128]{2,1,0:T(8,128)(2,1)S(1)}, u32[]{:S(2)}, u32[]{:S(2)}) async-start(bf16[64,8,128]{2,1,0:T(8,128)(2,1)} %shard_map.100), calls=%async_computation | async-start | bytes 262144 | tf_op jit(solution)/shard_map/all_to_all | solution.py:22
  70.1 0.0 collective-permute-done.5
  70.1 0.0 collective-permute-done.4
  70.1 0.0 collective-permute-done.3
  70.1 0.1 pad_maximum_fusion.kept
  70.3 1.9 %collective-permute-start.6 = (bf16[4,1024,128]{2,1,0:T(8,128)(2,1)S(1)}, bf16[4,1024,128]{2,1,0:T(8,128)(2,1)S(1)}, u32[]{:S(2)}, u32[]{:S(2)}) collective-permute-start(bf16[4,1024,128]{2,1,0:T(8,128)(2,1)S(1)} %pad_maximum_fusion.kept), channel_id=1, source_target_pairs={{0,64},{64,0},{1,65},{65,1},{2,66},{66,2},{3,67},{67,3},{4,68},{68... | collective-permute-start | bytes 3145736 | tf_op jit(solution)/shard_map/ppermute | solution.py:228
  72.2 13.0 %all-to-all-done.shares = bf16[64,8,128]{2,1,0:T(8,128)(2,1)S(1)} async-done(((bf16[64,8,128]{2,1,0:T(8,128)(2,1)}), bf16[64,8,128]{2,1,0:T(8,128)(2,1)S(1)}, u32[]{:S(2)}, u32[]{:S(2)}) %all-to-all-start) | async-done | bytes 131104 | tf_op jit(solution)/shard_map/all_to_all | solution.py:22
  85.2 0.7 shard_map.101
  86.0 20.6 %all_to_all.25 = bf16[64,8,128]{2,1,0:T(8,128)(2,1)S(1)} all-to-all(bf16[64,8,128]{2,1,0:T(8,128)(2,1)} %shard_map.101), channel_id=1, replica_groups=mesh['zh'=2,'x'=4,'core'=2,'y'=8,'z'=8] {'y','z'}, dimensions={0} | all-to-all | bytes 262144 | tf_op jit(solution)/shard_map/all_to_all | solution.py:22
  106.5 2.0 %shard_map.102 = (f32[128,128]{1,0:T(8,128)}, bf16[16,24,128]{2,1,0:T(8,128)(2,1)}) custom-call(bf16[512,128]{1,0:T(8,128)(2,1)S(1)} %bitcast.15, bf16[128,128]{1,0:T(8,128)(2,1)} %conv.5, bf16[256,128]{1,0:T(8,128)(2,1)} %dt_weight.1, f32[1,128]{1,0:T(1,128)} %bitcast.27, f32[16,128]{1,0:T(8,128)} %bitcast.23), custom_call_target="tpu_custom_call" | custom-call | tf_op jit(solution)/shard_map/pallas_call | solution.py:232
  108.6 10.2 %all-to-all-start.2 = ((bf16[16,24,128]{2,1,0:T(8,128)(2,1)}), bf16[16,24,128]{2,1,0:T(8,128)(2,1)S(1)}, u32[]{:S(2)}, u32[]{:S(2)}) async-start(bf16[16,24,128]{2,1,0:T(8,128)(2,1)} %get-tuple-element.12), calls=%async_computation.2 | async-start | bytes 196608 | tf_op jit(solution)/shard_map/all_to_all | solution.py:22
  118.8 0.6 pad_add_fusion.here
  119.3 2.3 %shard_map.103 = (f32[128,128]{1,0:T(8,128)}, f32[128,128]{1,0:T(8,128)}) custom-call(f32[128,128]{1,0:T(8,128)} %get-tuple-element.9.step_in, bf16[512,128]{1,0:T(8,128)(2,1)S(1)} %bitcast.16, bf16[128,128]{1,0:T(8,128)(2,1)} %conv.5, f32[16,128]{1,0:T(8,128)} %bitcast.24, f32[1,128]{1,0:T(1,128)} %bitcast.28), custom_call_target="tpu_custom_call" | custom-call | tf_op jit(solution)/shard_map/pallas_call | solution.py:237
  121.7 0.0 collective-permute-done.6.swapped
  121.7 2.7 %shard_map.104.gate_pre = f32[128,128]{1,0:T(8,128)} custom-call(s32[3]{0:T(128)} %pad_add_fusion.here, bf16[128,4096]{1,0:T(8,128)(2,1)} %hidden.1, bf16[4,1024,128]{2,1,0:T(8,128)(2,1)S(1)} %pad_maximum_fusion.kept, bf16[4,1024,128]{2,1,0:T(8,128)(2,1)S(1)} %collective-permute-done.6.swapped), custom_call_target="tpu_custom_call" | custom-call | tf_op jit(solution)/shard_map/pallas_call | solution.py:240
  124.3 7.5 %all-to-all-done.2.gathered = bf16[16,24,128]{2,1,0:T(8,128)(2,1)S(1)} async-done(((bf16[16,24,128]{2,1,0:T(8,128)(2,1)}), bf16[16,24,128]{2,1,0:T(8,128)(2,1)S(1)}, u32[]{:S(2)}, u32[]{:S(2)}) %all-to-all-start.2) | async-done | bytes 98336 | tf_op jit(solution)/shard_map/all_to_all | solution.py:22
  131.9 2.3 %shard_map.105 = bf16[8,128,128]{2,1,0:T(8,128)(2,1)} custom-call(s32[1]{0:T(128)} %bitcast.3.pos, f32[128,128]{1,0:T(8,128)} %get-tuple-element.10.through, f32[128,128]{1,0:T(8,128)} %get-tuple-element.11.local, bf16[512,128]{1,0:T(8,128)(2,1)S(1)} %bitcast.17, f32[16,128]{1,0:T(8,128)} %bitcast.25, f32[16,128]{1,0:T(8,128)} %bitcast.26, ...), custom_call_target="tpu_custom_call" | custom-call | tf_op jit(solution)/shard_map/pallas_call | solution.py:243
  134.1 15.7 %all_to_all.26.gated = bf16[8,128,128]{2,1,0:T(8,128)(2,1)S(1)} all-to-all(bf16[8,128,128]{2,1,0:T(8,128)(2,1)} %shard_map.105), channel_id=1, replica_groups=mesh['zh'=2,'x'=4,'core'=2,'y'=8,'z'=8] {'y'}, dimensions={0} | all-to-all | bytes 524288 | tf_op jit(solution)/shard_map/all_to_all | solution.py:22
  149.9 1.8 %shard_map.106 = bf16[64,8,128]{2,1,0:T(8,128)(2,1)} custom-call(s32[3]{0:T(128)} %pad_add_fusion.here, bf16[8,128,128]{2,1,0:T(8,128)(2,1)S(1)} %all_to_all.26.gated, bf16[4,1024,128]{2,1,0:T(8,128)(2,1)S(1)} %pad_maximum_fusion.kept, bf16[4,1024,128]{2,1,0:T(8,128)(2,1)S(1)} %copy-done.1), custom_call_target="tpu_custom_call" | custom-call | tf_op jit(solution)/shard_map/pallas_call | solution.py:254
  151.7 22.1 %all_to_all.27.shares = bf16[64,8,128]{2,1,0:T(8,128)(2,1)S(1)} all-to-all(bf16[64,8,128]{2,1,0:T(8,128)(2,1)} %shard_map.106), channel_id=1, replica_groups=mesh['zh'=2,'x'=4,'core'=2,'y'=8,'z'=8] {'y','z'}, dimensions={0} | all-to-all | bytes 262144 | tf_op jit(solution)/shard_map/all_to_all | solution.py:22
  173.8 0.7 shard_map.107
  (7 shorter events, 0.0 us)
Async XLA Ops:
  0.0 44.0 %collective-permute-start.2 = (bf16[256,128]{1,0:T(8,128)(2,1)}, bf16[256,128]{1,0:T(8,128)(2,1)S(1)}, u32[]{:S(2)}, u32[]{:S(2)}) collective-permute-start(bf16[256,128]{1,0:T(8,128)(2,1)} %param.19), channel_id=1, source_target_pairs={{0,512},{8,640},{16,768},{24,896},{32,0},{40,128},{48,256},{56,384... | collective-permute-start | bytes 196616 | tf_op jit(solution)/shard_map/ppermute | solution.py:210
  22.3 21.7 %collective-permute-start.1 = (bf16[256,128]{1,0:T(8,128)(2,1)}, bf16[256,128]{1,0:T(8,128)(2,1)S(1)}, u32[]{:S(2)}, u32[]{:S(2)}) collective-permute-start(bf16[256,128]{1,0:T(8,128)(2,1)} %param.19), channel_id=1, source_target_pairs={{0,0},{8,128},{16,256},{24,384},{32,512},{40,640},{48,768},{56,896... | collective-permute-start | bytes 196616 | tf_op jit(solution)/shard_map/ppermute | solution.py:209
  26.6 17.4 %collective-permute-start = (bf16[256,128]{1,0:T(8,128)(2,1)}, bf16[256,128]{1,0:T(8,128)(2,1)S(1)}, u32[]{:S(2)}, u32[]{:S(2)}) collective-permute-start(bf16[256,128]{1,0:T(8,128)(2,1)} %param.13), channel_id=1, source_target_pairs={{0,512},{512,0},{1,513},{513,1},{2,514},{514,2},{3,515},{515,3},{4... | collective-permute-start | bytes 196616 | tf_op jit(solution)/shard_map/ppermute | solution.py:208
  44.1 26.0 %collective-permute-start.5 = (bf16[1024,128]{1,0:T(8,128)(2,1)S(1)}, bf16[1024,128]{1,0:T(8,128)(2,1)S(1)}, u32[]{:S(2)}, u32[]{:S(2)}) collective-permute-start(bf16[1024,128]{1,0:T(8,128)(2,1)S(1)} %constant_dynamic-update-slice_fusion), channel_id=1, source_target_pairs={{0,384},{128,0},{256,128},{384,256},{1,385},{129,1},{257,129},{385... | collective-permute-start | bytes 786440 | tf_op jit(solution)/shard_map/ppermute | solution.py:226
  46.0 24.1 %collective-permute-start.4 = (bf16[1024,128]{1,0:T(8,128)(2,1)S(1)}, bf16[1024,128]{1,0:T(8,128)(2,1)S(1)}, u32[]{:S(2)}, u32[]{:S(2)}) collective-permute-start(bf16[1024,128]{1,0:T(8,128)(2,1)S(1)} %constant_dynamic-update-slice_fusion), channel_id=1, source_target_pairs={{0,256},{128,384},{256,0},{384,128},{1,257},{129,385},{257,1},{385... | collective-permute-start | bytes 786440 | tf_op jit(solution)/shard_map/ppermute | solution.py:226
  47.9 22.2 %collective-permute-start.3 = (bf16[1024,128]{1,0:T(8,128)(2,1)S(1)}, bf16[1024,128]{1,0:T(8,128)(2,1)S(1)}, u32[]{:S(2)}, u32[]{:S(2)}) collective-permute-start(bf16[1024,128]{1,0:T(8,128)(2,1)S(1)} %constant_dynamic-update-slice_fusion), channel_id=1, source_target_pairs={{0,128},{128,256},{256,384},{384,0},{1,129},{129,257},{257,385},{3... | collective-permute-start | bytes 786440 | tf_op jit(solution)/shard_map/ppermute | solution.py:226
  54.8 30.5 %all-to-all-start = ((bf16[64,8,128]{2,1,0:T(8,128)(2,1)}), bf16[64,8,128]{2,1,0:T(8,128)(2,1)S(1)}, u32[]{:S(2)}, u32[]{:S(2)}) async-start(bf16[64,8,128]{2,1,0:T(8,128)(2,1)} %shard_map.100), calls=%async_computation | async-start | bytes 262144 | tf_op jit(solution)/shard_map/all_to_all | solution.py:22
  70.3 51.4 %collective-permute-start.6 = (bf16[4,1024,128]{2,1,0:T(8,128)(2,1)S(1)}, bf16[4,1024,128]{2,1,0:T(8,128)(2,1)S(1)}, u32[]{:S(2)}, u32[]{:S(2)}) collective-permute-start(bf16[4,1024,128]{2,1,0:T(8,128)(2,1)S(1)} %pad_maximum_fusion.kept), channel_id=1, source_target_pairs={{0,64},{64,0},{1,65},{65,1},{2,66},{66,2},{3,67},{67,3},{4,68},{68... | collective-permute-start | bytes 3145736 | tf_op jit(solution)/shard_map/ppermute | solution.py:228
  108.6 23.3 %all-to-all-start.2 = ((bf16[16,24,128]{2,1,0:T(8,128)(2,1)}), bf16[16,24,128]{2,1,0:T(8,128)(2,1)S(1)}, u32[]{:S(2)}, u32[]{:S(2)}) async-start(bf16[16,24,128]{2,1,0:T(8,128)(2,1)} %get-tuple-element.12), calls=%async_computation.2 | async-start | bytes 196608 | tf_op jit(solution)/shard_map/all_to_all | solution.py:22
  121.7 2.7 %copy-start = (bf16[4,1024,128]{2,1,0:T(8,128)(2,1)}, bf16[4,1024,128]{2,1,0:T(8,128)(2,1)S(1)}, u32[]{:S(2)}) copy-start(bf16[4,1024,128]{2,1,0:T(8,128)(2,1)S(1)} %collective-permute-done.6.swapped) | copy-start | bytes 3145732
  131.9 18.0 %copy-start.1 = (bf16[4,1024,128]{2,1,0:T(8,128)(2,1)S(1)}, bf16[4,1024,128]{2,1,0:T(8,128)(2,1)}, u32[]{:S(2)}) copy-start(bf16[4,1024,128]{2,1,0:T(8,128)(2,1)} %copy-done) | copy-start | bytes 3145732

commit v2 on v1

--- a/solution.py
+++ b/solution.py
@@ -73,10 +73,28 @@
     for t in range(rows):
         state = jnp.exp2(step[t : t + 1] * rate) * state + driven[t : t + 1] * coef[:, t : t + 1]
     total = jnp.sum(step, axis=0, keepdims=True)
-    high = total.astype(jnp.bfloat16).astype(jnp.float32)
-    rest = jnp.zeros((PAYLOAD - STATE - 2, step.shape[1]), jnp.float32)
-    payload = jnp.concatenate([state, high, total - high, rest], axis=0).astype(jnp.bfloat16)
+    rest = jnp.broadcast_to(total, (PAYLOAD - STATE, step.shape[1]))
+    payload = jnp.concatenate([state, rest], axis=0)
     pay_out[...] = jnp.broadcast_to(payload[None], pay_out.shape)
+
+
+def chain_kernel(pos, a_log, gathered, all_out, own_out):
+    rate = -jnp.exp(a_log[...]) * LOG2E
+    state = jnp.zeros(rate.shape, jnp.float32)
+    total = jnp.zeros((1, rate.shape[1]), jnp.float32)
+    rest = PAYLOAD - STATE
+    for source in range(gathered.shape[0]):
+
+        @pl.when(pos[0] == source)
+        def _(state=state, total=total):
+            own_out[:STATE] = state
+            own_out[STATE:] = jnp.broadcast_to(total, (rest, total.shape[1]))
+
+        step = gathered[source, STATE : STATE + 1]
+        state = jnp.exp2(step * rate) * state + gathered[source, :STATE]
+        total = total + step
+    all_out[:STATE] = state
+    all_out[STATE:] = jnp.broadcast_to(total, (rest, total.shape[1]))
 
 
 def gate_kernel(here, hidden, kept, swapped, out):
@@ -90,7 +108,7 @@
                 at = (line * 2 + (here[2] + other) % 2) * block
                 total += jnp.dot(
                     hidden[:, pl.ds(pl.multiple_of(at, block), block)],
-                    weight[back, turn * block : (turn + 1) * block],
+                    weight[back, 2 * turn * block : (2 * turn + 1) * block],
                     preferred_element_type=jnp.float32,
                 )
     out[...] = total
@@ -115,15 +133,12 @@
         out[t : t + 1] = value + direct[t : t + 1]
 
 
-def gated_kernel(pos, through, local, proj, a_log, state_in, gathered, gate_pre, out, carried):
+def gated_kernel(through, local, proj, a_log, state_in, half, before, gate_pre, out, carried):
     rows = local.shape[0]
     rate = -jnp.exp(a_log[...]) * LOG2E
     state = state_in[...]
-    for source in range(gathered.shape[0]):
-        payload = gathered[source].astype(jnp.float32)
-        total = payload[STATE : STATE + 1] + payload[STATE + 1 : STATE + 2]
-        moved = jnp.exp2(total * rate) * state + payload[:STATE]
-        state = jnp.where(source < pos[0], moved, state)
+    for part in (half, before):
+        state = jnp.exp2(part[STATE : STATE + 1] * rate) * state + part[:STATE]
     coefs = coefficients(proj, RANK + STATE, STATE)
     for t in range(rows):
         left = jnp.exp2(through[t : t + 1] * rate) * state
@@ -147,7 +162,7 @@
                 line = (here[0] + turn) % 2 * n_x + (here[1] + n_x - back) % n_x
                 part += lax.dot_general(
                     gated[line],
-                    weight[back, (2 + turn) * block : (3 + turn) * block],
+                    weight[back, (2 * turn + 1) * block : (2 * turn + 2) * block],
                     (((1,), (1,)), ((), ())),
                     preferred_element_type=jnp.float32,
                 )
@@ -180,16 +195,16 @@
 
 def shards_for(sizes):
     n_zh, n_x, n_core, n_y, n_z = sizes
-    n_f, n_c = n_zh * n_x * n_core, n_y * n_z
-
-    def turned(flip):
+    n_c = n_y * n_z
+
+    def turned():
         pairs = []
         for zh in range(n_zh):
             for x in range(n_x):
                 for core in range(n_core):
                     for y in range(n_y):
                         source = ((zh * n_x + x) * n_core + core) * n_y + y
-                        to_zh, to_x = (y // n_x + flip) % n_zh, y % n_x
+                        to_zh, to_x = y // n_x, y % n_x
                         target = ((to_zh * n_x + to_x) * n_core + core) * n_y + zh * n_x + x
                         pairs.append((source, target))
         return pairs
@@ -201,17 +216,17 @@
         own = rows // n_c
         here = jnp.stack([lax.axis_index(axis) for axis in FSDP]).astype(jnp.int32)
         own_piece = lax.axis_index(CHAN).astype(jnp.int32)[None]
-        position = lax.axis_index(FSDP).astype(jnp.int32)[None]
+        position = lax.axis_index(("x", "core")).astype(jnp.int32)[None]
         bf16, f32 = jnp.bfloat16, jnp.float32
-        shape = jax.ShapeDtypeStruct
-
-        gate_far = lax.ppermute(gate_weight, "zh", [(0, 1), (1, 0)])
-        out_near = lax.ppermute(out_weight, FSDP + ("y",), turned(0))
-        out_far = lax.ppermute(out_weight, FSDP + ("y",), turned(1))
+        shape, near = jax.ShapeDtypeStruct, pltpu.VMEM
+
+        turned_weight = lax.ppermute(out_weight, FSDP + ("y",), turned())
+        pair = jnp.concatenate([gate_weight, turned_weight], axis=0)
+        far = lax.ppermute(pair, "zh", [(0, 1), (1, 0)])
 
         used = xproj_weight.shape[1] + 2 * STATE
         piece = -(-used // (8 * n_c)) * 8
-        shares = pl.pallas_call(project_kernel, out_shape=shape((n_c, piece, rows), bf16))(
+        shares = pl.pallas_call(project_kernel, out_shape=near((n_c, piece, rows), bf16))(
             xproj_weight.T, conv_out
         )
         shares = exchange(shares, CHAN)
@@ -220,7 +235,7 @@
         )(own_piece, near_core(shares))
         proj = exchange(summed, CHAN).reshape(n_c * piece, rows)
 
-        mine = jnp.concatenate([gate_weight, gate_far, out_near, out_far], axis=0)
+        mine = jnp.concatenate([pair, far], axis=0)
         kept = [mine]
         for back in range(1, n_x):
             kept.append(lax.ppermute(mine, "x", [(i, (i + back) % n_x) for i in range(n_x)]))
@@ -231,21 +246,35 @@
         proj, log_rate = near_core(proj), a_log.T
         step, payload = pl.pallas_call(
             local_kernel,
-            out_shape=(shape((rows, channels), f32), shape((n_f, PAYLOAD, channels), bf16)),
+            out_shape=(near((rows, channels), f32), near((n_x * n_core, PAYLOAD, channels), f32)),
         )(proj, conv_out, dt_weight, dt_bias[None], log_rate)
-        gathered = near_core(exchange(payload, FSDP))
+        gathered = near_core(exchange(payload, ("x", "core")))
+        half, before = pl.pallas_call(
+            chain_kernel,
+            in_specs=[SMEM, VMEM, VMEM],
+            out_shape=(near((PAYLOAD, channels), f32),) * 2,
+        )(position, log_rate, gathered)
+        half = near_core(lax.ppermute(half, "zh", [(0, 1)]))
         local, through = pl.pallas_call(
-            scan_kernel, out_shape=(shape((rows, channels), f32),) * 2
-        )(step, proj, conv_out, log_rate, skip_gain[None])
+            scan_kernel, out_shape=(near((rows, channels), f32),) * 2
+        )(near_core(step), proj, conv_out, log_rate, skip_gain[None])
         gate_pre = pl.pallas_call(
-            gate_kernel, in_specs=[SMEM] + [VMEM] * 3, out_shape=shape((rows, channels), f32)
+            gate_kernel, in_specs=[SMEM] + [VMEM] * 3, out_shape=near((rows, channels), f32)
         )(here, hidden, kept, swapped)
         gated = pl.pallas_call(
             gated_kernel,
-            in_specs=[SMEM] + [VMEM] * 7,
-            out_shape=shape((n_y, rows, channels), bf16),
+            out_shape=near((n_y, rows, channels), bf16),
             scratch_shapes=[pltpu.VMEM((rows, channels), f32)],
-        )(position, through, local, proj, log_rate, state_in.T, gathered, gate_pre)
+        )(
+            near_core(through),
+            near_core(local),
+            proj,
+            log_rate,
+            state_in.T,
+            half,
+            near_core(before),
+            near_core(gate_pre),
+        )
         line = near_core(exchange(gated, "y"))
 
         width = hidden.shape[1] // n_y
@@ -254,7 +283,7 @@
         sums = pl.pallas_call(
             mix_kernel,
             in_specs=[SMEM] + [VMEM] * 3,
-            out_shape=shape((n_c, own * tiles, lanes), bf16),
+            out_shape=near((n_c, own * tiles, lanes), bf16),
             scratch_shapes=[
                 pltpu.VMEM((tiles, rows, lanes), f32),
                 pltpu.VMEM((rows * tiles, lanes), f32),

time: 176 us -> 179 us (1.017)
  starting transfers between devices: 65 us -> 78 us
  waiting for transfers between devices: 35.1 us -> 30.7 us
  blocking collectives: 58.4 us -> 54.5 us
  Pallas kernels: 14.2 us -> 12.1 us
    ppermute x3, starting transfers between devices: 28.5 us -> 46.9 us  [the longest x1 29.6 us: shards(): far = lax.ppermute(pair, 'zh', [(0, 1), (1, 0)])]
    all_to_all x2, starting transfers between devices: 25.5 us -> 17.5 us  [exchange(): return lax.all_to_all(array, axes, 0, 0, tiled=True)]
    all_to_all x3, blocking collectives: 58.4 us -> 54.5 us  [exchange(): return lax.all_to_all(array, axes, 0, 0, tiled=True)]
    all_to_all x2, waiting for transfers between devices: 20.5 us -> 17.4 us  [exchange(): return lax.all_to_all(array, axes, 0, 0, tiled=True)]
    ppermute x3, starting transfers between devices: 8.97 us -> 11.7 us  [shards(): lax.ppermute(mine, 'x', [(i, (i + back) % n_x) for i in range(n_x)])]
    pallas_call x6 -> x7, Pallas kernels: 12.9 us -> 10.7 us  [the longest x1 2.06 us: shards(): pl.pallas_call(local_kernel, out_shape=(near((rows, channels), f32), near...]
  transfers between devices with their start and end apart: 9 -> 9, of which waited for: 3 -> 4; matrix products, arithmetic and copies ran while one was open for 1% -> 0% of each run, Pallas kernels for 5% -> 5%
where the time goes in v2:
time: 179 us; the launch traced here: 177 us
  starting transfers between devices  78 us (44%)
  blocking collectives  54.5 us (30%)
  waiting for transfers between devices  30.7 us (17%)
  Pallas kernels  12.1 us (7%)
    all_to_all x3, blocking collectives, exchange(): return lax.all_to_all(array, axes, 0, 0, tiled=True)  54.5 us
    ppermute x1, starting transfers between devices, shards(): far = lax.ppermute(pair, 'zh', [(0, 1), (1, 0)])  29.6 us
    all_to_all x2, starting transfers between devices, exchange(): return lax.all_to_all(array, axes, 0, 0, tiled=True)  17.5 us
    all_to_all x2, waiting for transfers between devices, exchange(): return lax.all_to_all(array, axes, 0, 0, tiled=True)  17.4 us
    ppermute x3, starting transfers between devices, shards(): lax.ppermute(mine, 'x', [(i, (i + back) % n_x) for i in range(n_x)])  11.7 us
    ppermute x1, starting transfers between devices, shards(): half = near_core(lax.ppermute(half, 'zh', [(0, 1)]))  11.7 us
    ppermute x1, waiting for transfers between devices, shards(): far = lax.ppermute(pair, 'zh', [(0, 1), (1, 0)])  8.46 us
    ppermute x1, starting transfers between devices, shards(): turned_weight = lax.ppermute(out_weight, FSDP + ('y',), turned())  5.54 us
  transfers between devices with their start and end apart: 9, of which 4 were waited for; matrix products, arithmetic and copies ran while one was open for 0% of the time, Pallas kernels for 5%

profile of v2, /device:TPU:6, one launch (start us, length us, event | category | flops | bytes accessed | tf_op | source)
XLA Modules:
  0.0 177.2 jit_solution(4070187330301966805)
XLA Ops:
  0.0 5.5 %collective-permute-start.1 = (bf16[256,128]{1,0:T(8,128)(2,1)}, bf16[256,128]{1,0:T(8,128)(2,1)S(1)}, u32[]{:S(2)}, u32[]{:S(2)}) collective-permute-start(bf16[256,128]{1,0:T(8,128)(2,1)} %param.19), channel_id=1, source_target_pairs={{0,0},{8,128},{16,256},{24,384},{32,512},{40,640},{48,768},{56,896... | collective-permute-start | bytes 196616 | tf_op jit(solution)/shard_map/ppermute | solution.py:223
  5.6 4.8 %collective-permute-done.1 = bf16[256,128]{1,0:T(8,128)(2,1)S(1)} collective-permute-done((bf16[256,128]{1,0:T(8,128)(2,1)}, bf16[256,128]{1,0:T(8,128)(2,1)S(1)}, u32[]{:S(2)}, u32[]{:S(2)}) %collective-permute-start.1) | collective-permute-done | bytes 65568 | tf_op jit(solution)/shard_map/ppermute | solution.py:223
  10.4 0.8 pad_maximum_fusion.1
  11.3 29.6 %collective-permute-start.2 = (bf16[512,128]{1,0:T(8,128)(2,1)S(1)}, bf16[512,128]{1,0:T(8,128)(2,1)S(1)}, u32[]{:S(2)}, u32[]{:S(2)}) collective-permute-start(bf16[512,128]{1,0:T(8,128)(2,1)S(1)} %pad_maximum_fusion.1), channel_id=1, source_target_pairs={{0,512},{512,0},{1,513},{513,1},{2,514},{514,2},{3,515},{515,3},{4... | collective-permute-start | bytes 393224 | tf_op jit(solution)/shard_map/ppermute | solution.py:225
  41.0 8.5 %collective-permute-done.2 = bf16[512,128]{1,0:T(8,128)(2,1)S(1)} collective-permute-done((bf16[512,128]{1,0:T(8,128)(2,1)S(1)}, bf16[512,128]{1,0:T(8,128)(2,1)S(1)}, u32[]{:S(2)}, u32[]{:S(2)}) %collective-permute-start.2) | collective-permute-done | bytes 131104 | tf_op jit(solution)/shard_map/ppermute | solution.py:225
  49.4 5.2 %collective-permute-start.5 = (bf16[1024,128]{1,0:T(8,128)(2,1)S(1)}, bf16[1024,128]{1,0:T(8,128)(2,1)S(1)}, u32[]{:S(2)}, u32[]{:S(2)}) collective-permute-start(bf16[1024,128]{1,0:T(8,128)(2,1)S(1)} %constant_dynamic-update-slice_fusion), channel_id=1, source_target_pairs={{0,384},{128,0},{256,128},{384,256},{1,385},{129,1},{257,129},{385... | collective-permute-start | bytes 786440 | tf_op jit(solution)/shard_map/ppermute | solution.py:241
  54.7 2.2 %collective-permute-start.4 = (bf16[1024,128]{1,0:T(8,128)(2,1)S(1)}, bf16[1024,128]{1,0:T(8,128)(2,1)S(1)}, u32[]{:S(2)}, u32[]{:S(2)}) collective-permute-start(bf16[1024,128]{1,0:T(8,128)(2,1)S(1)} %constant_dynamic-update-slice_fusion), channel_id=1, source_target_pairs={{0,256},{128,384},{256,0},{384,128},{1,257},{129,385},{257,1},{385... | collective-permute-start | bytes 786440 | tf_op jit(solution)/shard_map/ppermute | solution.py:241
  56.9 4.3 %collective-permute-start.3 = (bf16[1024,128]{1,0:T(8,128)(2,1)S(1)}, bf16[1024,128]{1,0:T(8,128)(2,1)S(1)}, u32[]{:S(2)}, u32[]{:S(2)}) collective-permute-start(bf16[1024,128]{1,0:T(8,128)(2,1)S(1)} %constant_dynamic-update-slice_fusion), channel_id=1, source_target_pairs={{0,128},{128,256},{256,384},{384,0},{1,129},{129,257},{257,385},{3... | collective-permute-start | bytes 786440 | tf_op jit(solution)/shard_map/ppermute | solution.py:241
  61.2 1.7 shard_map.100
  62.9 13.0 %all-to-all-start = ((bf16[64,8,128]{2,1,0:T(8,128)(2,1)}), bf16[64,8,128]{2,1,0:T(8,128)(2,1)S(1)}, u32[]{:S(2)}, u32[]{:S(2)}) async-start(bf16[64,8,128]{2,1,0:T(8,128)(2,1)} %shard_map.100), calls=%async_computation | async-start | bytes 262144 | tf_op jit(solution)/shard_map/all_to_all | solution.py:22
  75.9 0.0 collective-permute-done.5
  75.9 0.0 collective-permute-done.4
  75.9 0.0 collective-permute-done.3
  75.9 0.1 pad_maximum_fusion.kept
  76.1 1.9 %collective-permute-start.6 = (bf16[4,1024,128]{2,1,0:T(8,128)(2,1)S(1)}, bf16[4,1024,128]{2,1,0:T(8,128)(2,1)S(1)}, u32[]{:S(2)}, u32[]{:S(2)}) collective-permute-start(bf16[4,1024,128]{2,1,0:T(8,128)(2,1)S(1)} %pad_maximum_fusion.kept), channel_id=1, source_target_pairs={{0,64},{64,0},{1,65},{65,1},{2,66},{66,2},{3,67},{67,3},{4,68},{68... | collective-permute-start | bytes 3145736 | tf_op jit(solution)/shard_map/ppermute | solution.py:243
  78.0 13.7 %all-to-all-done.shares = bf16[64,8,128]{2,1,0:T(8,128)(2,1)S(1)} async-done(((bf16[64,8,128]{2,1,0:T(8,128)(2,1)}), bf16[64,8,128]{2,1,0:T(8,128)(2,1)S(1)}, u32[]{:S(2)}, u32[]{:S(2)}) %all-to-all-start) | async-done | bytes 131104 | tf_op jit(solution)/shard_map/all_to_all | solution.py:22
  91.7 0.7 shard_map.101
  92.4 20.8 %all_to_all.25 = bf16[64,8,128]{2,1,0:T(8,128)(2,1)S(1)} all-to-all(bf16[64,8,128]{2,1,0:T(8,128)(2,1)} %shard_map.101), channel_id=1, replica_groups=mesh['zh'=2,'x'=4,'core'=2,'y'=8,'z'=8] {'y','z'}, dimensions={0} | all-to-all | bytes 262144 | tf_op jit(solution)/shard_map/all_to_all | solution.py:22
  113.3 2.1 %shard_map.102 = (f32[128,128]{1,0:T(8,128)S(1)}, f32[8,24,128]{2,1,0:T(8,128)}) custom-call(bf16[512,128]{1,0:T(8,128)(2,1)S(1)} %bitcast.15, bf16[128,128]{1,0:T(8,128)(2,1)} %conv.5, bf16[256,128]{1,0:T(8,128)(2,1)} %dt_weight.1, f32[1,128]{1,0:T(1,128)} %bitcast.28, f32[16,128]{1,0:T(8,128)} %bitcast.22), custom_call_target="tpu_custom_call" | custom-call | tf_op jit(solution)/shard_map/pallas_call | solution.py:247
  115.3 4.5 %all-to-all-start.2 = ((f32[8,24,128]{2,1,0:T(8,128)}), f32[8,24,128]{2,1,0:T(8,128)S(1)}, u32[]{:S(2)}, u32[]{:S(2)}) async-start(f32[8,24,128]{2,1,0:T(8,128)} %get-tuple-element.14), calls=%async_computation.2 | async-start | bytes 196608 | tf_op jit(solution)/shard_map/all_to_all | solution.py:22
  119.8 3.7 %all-to-all-done.2.gathered = f32[8,24,128]{2,1,0:T(8,128)S(1)} async-done(((f32[8,24,128]{2,1,0:T(8,128)}), f32[8,24,128]{2,1,0:T(8,128)S(1)}, u32[]{:S(2)}, u32[]{:S(2)}) %all-to-all-start.2) | async-done | bytes 98336 | tf_op jit(solution)/shard_map/all_to_all | solution.py:22
  123.6 0.8 shard_map.104
  124.4 11.7 %collective-permute-start = (f32[24,128]{1,0:T(8,128)S(1)}, f32[24,128]{1,0:T(8,128)S(1)}, u32[]{:S(2)}, u32[]{:S(2)}) collective-permute-start(f32[24,128]{1,0:T(8,128)S(1)} %get-tuple-element.15), channel_id=1, source_target_pairs={{0,512},{1,513},{2,514},{3,515},{4,516},{5,517},{6,518},{7,519},{8... | collective-permute-start | bytes 36872 | tf_op jit(solution)/shard_map/ppermute | solution.py:257
  136.0 0.6 pad_add_fusion.here
  136.6 1.6 shard_map.103
  138.2 0.0 collective-permute-done.6.swapped
  138.3 2.0 %shard_map.105.gate_pre = f32[128,128]{1,0:T(8,128)S(1)} custom-call(s32[3]{0:T(128)} %pad_add_fusion.here, bf16[128,4096]{1,0:T(8,128)(2,1)} %hidden.1, bf16[4,1024,128]{2,1,0:T(8,128)(2,1)S(1)} %pad_maximum_fusion.kept, bf16[4,1024,128]{2,1,0:T(8,128)(2,1)S(1)} %collective-permute-done.6.swapped), custom_call_target="tpu_custom_call" | custom-call | tf_op jit(solution)/shard_map/pallas_call | solution.py:261
  140.3 1.3 shard_map.106
  141.7 14.1 %all_to_all.26.gated = bf16[8,128,128]{2,1,0:T(8,128)(2,1)S(1)} all-to-all(bf16[8,128,128]{2,1,0:T(8,128)(2,1)S(1)} %shard_map.106), channel_id=1, replica_groups=mesh['zh'=2,'x'=4,'core'=2,'y'=8,'z'=8] {'y'}, dimensions={0} | all-to-all | bytes 524288 | tf_op jit(solution)/shard_map/all_to_all | solution.py:22
  155.8 1.2 shard_map.107
  157.0 19.5 %all_to_all.27.shares = bf16[64,8,128]{2,1,0:T(8,128)(2,1)S(1)} all-to-all(bf16[64,8,128]{2,1,0:T(8,128)(2,1)S(1)} %shard_map.107), channel_id=1, replica_groups=mesh['zh'=2,'x'=4,'core'=2,'y'=8,'z'=8] {'y','z'}, dimensions={0} | all-to-all | bytes 262144 | tf_op jit(solution)/shard_map/all_to_all | solution.py:22
  176.5 0.7 shard_map.108
  (10 shorter events, 0.1 us)
Async XLA Ops:
  0.0 40.9 %copy-start.2 = (bf16[256,128]{1,0:T(8,128)(2,1)S(1)}, bf16[256,128]{1,0:T(8,128)(2,1)}, u32[]{:S(2)}) copy-start(bf16[256,128]{1,0:T(8,128)(2,1)} %param.13) | copy-start | bytes 196612
  0.0 10.4 %collective-permute-start.1 = (bf16[256,128]{1,0:T(8,128)(2,1)}, bf16[256,128]{1,0:T(8,128)(2,1)S(1)}, u32[]{:S(2)}, u32[]{:S(2)}) collective-permute-start(bf16[256,128]{1,0:T(8,128)(2,1)} %param.19), channel_id=1, source_target_pairs={{0,0},{8,128},{16,256},{24,384},{32,512},{40,640},{48,768},{56,896... | collective-permute-start | bytes 196616 | tf_op jit(solution)/shard_map/ppermute | solution.py:223
  11.3 38.2 %collective-permute-start.2 = (bf16[512,128]{1,0:T(8,128)(2,1)S(1)}, bf16[512,128]{1,0:T(8,128)(2,1)S(1)}, u32[]{:S(2)}, u32[]{:S(2)}) collective-permute-start(bf16[512,128]{1,0:T(8,128)(2,1)S(1)} %pad_maximum_fusion.1), channel_id=1, source_target_pairs={{0,512},{512,0},{1,513},{513,1},{2,514},{514,2},{3,515},{515,3},{4... | collective-permute-start | bytes 393224 | tf_op jit(solution)/shard_map/ppermute | solution.py:225
  49.4 26.5 %collective-permute-start.5 = (bf16[1024,128]{1,0:T(8,128)(2,1)S(1)}, bf16[1024,128]{1,0:T(8,128)(2,1)S(1)}, u32[]{:S(2)}, u32[]{:S(2)}) collective-permute-start(bf16[1024,128]{1,0:T(8,128)(2,1)S(1)} %constant_dynamic-update-slice_fusion), channel_id=1, source_target_pairs={{0,384},{128,0},{256,128},{384,256},{1,385},{129,1},{257,129},{385... | collective-permute-start | bytes 786440 | tf_op jit(solution)/shard_map/ppermute | solution.py:241
  54.7 21.2 %collective-permute-start.4 = (bf16[1024,128]{1,0:T(8,128)(2,1)S(1)}, bf16[1024,128]{1,0:T(8,128)(2,1)S(1)}, u32[]{:S(2)}, u32[]{:S(2)}) collective-permute-start(bf16[1024,128]{1,0:T(8,128)(2,1)S(1)} %constant_dynamic-update-slice_fusion), channel_id=1, source_target_pairs={{0,256},{128,384},{256,0},{384,128},{1,257},{129,385},{257,1},{385... | collective-permute-start | bytes 786440 | tf_op jit(solution)/shard_map/ppermute | solution.py:241
  56.9 19.0 %collective-permute-start.3 = (bf16[1024,128]{1,0:T(8,128)(2,1)S(1)}, bf16[1024,128]{1,0:T(8,128)(2,1)S(1)}, u32[]{:S(2)}, u32[]{:S(2)}) collective-permute-start(bf16[1024,128]{1,0:T(8,128)(2,1)S(1)} %constant_dynamic-update-slice_fusion), channel_id=1, source_target_pairs={{0,128},{128,256},{256,384},{384,0},{1,129},{129,257},{257,385},{3... | collective-permute-start | bytes 786440 | tf_op jit(solution)/shard_map/ppermute | solution.py:241
  62.9 28.8 %all-to-all-start = ((bf16[64,8,128]{2,1,0:T(8,128)(2,1)}), bf16[64,8,128]{2,1,0:T(8,128)(2,1)S(1)}, u32[]{:S(2)}, u32[]{:S(2)}) async-start(bf16[64,8,128]{2,1,0:T(8,128)(2,1)} %shard_map.100), calls=%async_computation | async-start | bytes 262144 | tf_op jit(solution)/shard_map/all_to_all | solution.py:22
  76.1 62.2 %collective-permute-start.6 = (bf16[4,1024,128]{2,1,0:T(8,128)(2,1)S(1)}, bf16[4,1024,128]{2,1,0:T(8,128)(2,1)S(1)}, u32[]{:S(2)}, u32[]{:S(2)}) collective-permute-start(bf16[4,1024,128]{2,1,0:T(8,128)(2,1)S(1)} %pad_maximum_fusion.kept), channel_id=1, source_target_pairs={{0,64},{64,0},{1,65},{65,1},{2,66},{66,2},{3,67},{67,3},{4,68},{68... | collective-permute-start | bytes 3145736 | tf_op jit(solution)/shard_map/ppermute | solution.py:243
  115.3 8.2 %all-to-all-start.2 = ((f32[8,24,128]{2,1,0:T(8,128)}), f32[8,24,128]{2,1,0:T(8,128)S(1)}, u32[]{:S(2)}, u32[]{:S(2)}) async-start(f32[8,24,128]{2,1,0:T(8,128)} %get-tuple-element.14), calls=%async_computation.2 | async-start | bytes 196608 | tf_op jit(solution)/shard_map/all_to_all | solution.py:22
  124.4 16.0 %collective-permute-start = (f32[24,128]{1,0:T(8,128)S(1)}, f32[24,128]{1,0:T(8,128)S(1)}, u32[]{:S(2)}, u32[]{:S(2)}) collective-permute-start(f32[24,128]{1,0:T(8,128)S(1)} %get-tuple-element.15), channel_id=1, source_target_pairs={{0,512},{1,513},{2,514},{3,515},{4,516},{5,517},{6,518},{7,519},{8... | collective-permute-start | bytes 36872 | tf_op jit(solution)/shard_map/ppermute | solution.py:257
  138.2 2.1 %copy-start = (bf16[4,1024,128]{2,1,0:T(8,128)(2,1)}, bf16[4,1024,128]{2,1,0:T(8,128)(2,1)S(1)}, u32[]{:S(2)}) copy-start(bf16[4,1024,128]{2,1,0:T(8,128)(2,1)S(1)} %collective-permute-done.6.swapped) | copy-start | bytes 3145732
  140.3 15.5 %copy-start.1 = (bf16[4,1024,128]{2,1,0:T(8,128)(2,1)S(1)}, bf16[4,1024,128]{2,1,0:T(8,128)(2,1)}, u32[]{:S(2)}) copy-start(bf16[4,1024,128]{2,1,0:T(8,128)(2,1)} %copy-done) | copy-start | bytes 3145732

commit v3 on v2

--- a/solution.py
+++ b/solution.py
@@ -13,9 +13,16 @@
 FSDP_CHAN = FSDP + CHAN
 SPLIT = {16: (2, 4, 2), 64: (8, 8)}
 PAYLOAD = 24
+GRANT = 16 << 20
 LOG2E = 1.4426950408889634
 VMEM = pl.BlockSpec(memory_space=pltpu.VMEM)
 SMEM = pl.BlockSpec(memory_space=pltpu.SMEM)
+
+
+def run(kernel, **settings):
+    if kernel in (gate_kernel, mix_kernel, chain_kernel, gated_kernel):
+        settings["compiler_params"] = pltpu.CompilerParams(vmem_limit_bytes=GRANT)
+    return pl.pallas_call(kernel, **settings)
 
 
 def exchange(array, axes):
@@ -97,15 +104,15 @@
     all_out[STATE:] = jnp.broadcast_to(total, (rest, total.shape[1]))
 
 
-def gate_kernel(here, hidden, kept, swapped, out):
+def gate_kernel(zh, x, core, hidden, kept, swapped, out):
     n_x, depth, _ = kept.shape
     block = depth // 4
     total = jnp.zeros(out.shape, jnp.float32)
     for other, weight in enumerate((kept, swapped)):
         for back in range(n_x):
             for turn in range(2):
-                line = (here[0] + turn) % 2 * n_x + (here[1] + n_x - back) % n_x
-                at = (line * 2 + (here[2] + other) % 2) * block
+                line = (zh[0] + turn) % 2 * n_x + (x[0] + n_x - back) % n_x
+                at = (line * 2 + (core[0] + other) % 2) * block
                 total += jnp.dot(
                     hidden[:, pl.ds(pl.multiple_of(at, block), block)],
                     weight[back, 2 * turn * block : (2 * turn + 1) * block],
@@ -148,7 +155,7 @@
     out[...] = jnp.broadcast_to(value.astype(jnp.bfloat16)[None], out.shape)
 
 
-def mix_kernel(here, gated, kept, swapped, out, total, staged):
+def mix_kernel(zh, x, core, gated, kept, swapped, out, total, staged):
     n_x, depth, _ = kept.shape
     block = depth // 4
     tiles, rows, lanes = total.shape
@@ -159,7 +166,7 @@
         part = jnp.zeros((rows, block), jnp.float32)
         for back in range(n_x):
             for turn in range(2):
-                line = (here[0] + turn) % 2 * n_x + (here[1] + n_x - back) % n_x
+                line = (zh[0] + turn) % 2 * n_x + (x[0] + n_x - back) % n_x
                 part += lax.dot_general(
                     gated[line],
                     weight[back, (2 * turn + 1) * block : (2 * turn + 2) * block],
@@ -167,7 +174,7 @@
                     preferred_element_type=jnp.float32,
                 )
         for k in range(per):
-            total[(here[2] + other) % 2 * per + k] = part[:, k * lanes : (k + 1) * lanes]
+            total[(core[0] + other) % 2 * per + k] = part[:, k * lanes : (k + 1) * lanes]
     for row in range(own):
         for tile in range(tiles):
             staged[pl.ds(row * tiles + tile, pieces, stride=height), :] = total[
@@ -214,28 +221,29 @@
     ):
         rows, channels = conv_out.shape
         own = rows // n_c
-        here = jnp.stack([lax.axis_index(axis) for axis in FSDP]).astype(jnp.int32)
+        here = [lax.axis_index(axis).astype(jnp.int32)[None] for axis in FSDP]
         own_piece = lax.axis_index(CHAN).astype(jnp.int32)[None]
         position = lax.axis_index(("x", "core")).astype(jnp.int32)[None]
         bf16, f32 = jnp.bfloat16, jnp.float32
         shape, near = jax.ShapeDtypeStruct, pltpu.VMEM
 
         turned_weight = lax.ppermute(out_weight, FSDP + ("y",), turned())
-        pair = jnp.concatenate([gate_weight, turned_weight], axis=0)
-        far = lax.ppermute(pair, "zh", [(0, 1), (1, 0)])
+        halves = [(0, 1), (1, 0)]
+        gate_far = lax.ppermute(gate_weight, "zh", halves)
+        turned_far = lax.ppermute(turned_weight, "zh", halves)
 
         used = xproj_weight.shape[1] + 2 * STATE
         piece = -(-used // (8 * n_c)) * 8
-        shares = pl.pallas_call(project_kernel, out_shape=near((n_c, piece, rows), bf16))(
+        shares = run(project_kernel, out_shape=near((n_c, piece, rows), bf16))(
             xproj_weight.T, conv_out
         )
         shares = exchange(shares, CHAN)
-        summed = pl.pallas_call(
+        summed = run(
             add_kernel, in_specs=[SMEM, VMEM], out_shape=shape(shares.shape, bf16)
         )(own_piece, near_core(shares))
         proj = exchange(summed, CHAN).reshape(n_c * piece, rows)
 
-        mine = jnp.concatenate([pair, far], axis=0)
+        mine = jnp.concatenate([gate_weight, turned_weight, gate_far, turned_far], axis=0)
         kept = [mine]
         for back in range(1, n_x):
             kept.append(lax.ppermute(mine, "x", [(i, (i + back) % n_x) for i in range(n_x)]))
@@ -244,24 +252,25 @@
         kept = near_core(kept)
 
         proj, log_rate = near_core(proj), a_log.T
-        step, payload = pl.pallas_call(
+        conv_near = conv_out
+        step, payload = run(
             local_kernel,
             out_shape=(near((rows, channels), f32), near((n_x * n_core, PAYLOAD, channels), f32)),
-        )(proj, conv_out, dt_weight, dt_bias[None], log_rate)
+        )(proj, conv_near, dt_weight, dt_bias[None], log_rate)
         gathered = near_core(exchange(payload, ("x", "core")))
-        half, before = pl.pallas_call(
+        half, before = run(
             chain_kernel,
             in_specs=[SMEM, VMEM, VMEM],
             out_shape=(near((PAYLOAD, channels), f32),) * 2,
         )(position, log_rate, gathered)
         half = near_core(lax.ppermute(half, "zh", [(0, 1)]))
-        local, through = pl.pallas_call(
+        local, through = run(
             scan_kernel, out_shape=(near((rows, channels), f32),) * 2
-        )(near_core(step), proj, conv_out, log_rate, skip_gain[None])
-        gate_pre = pl.pallas_call(
-            gate_kernel, in_specs=[SMEM] + [VMEM] * 3, out_shape=near((rows, channels), f32)
-        )(here, hidden, kept, swapped)
-        gated = pl.pallas_call(
+        )(near_core(step), proj, conv_near, log_rate, skip_gain[None])
+        gate_pre = run(
+            gate_kernel, in_specs=[SMEM] * 3 + [VMEM] * 3, out_shape=near((rows, channels), f32)
+        )(*here, hidden, kept, swapped)
+        gated = run(
             gated_kernel,
             out_shape=near((n_y, rows, channels), bf16),
             scratch_shapes=[pltpu.VMEM((rows, channels), f32)],
@@ -280,17 +289,17 @@
         width = hidden.shape[1] // n_y
         lanes = min(128, width // n_core)
         tiles = width // lanes
-        sums = pl.pallas_call(
+        sums = run(
             mix_kernel,
-            in_specs=[SMEM] + [VMEM] * 3,
+            in_specs=[SMEM] * 3 + [VMEM] * 3,
             out_shape=near((n_c, own * tiles, lanes), bf16),
             scratch_shapes=[
                 pltpu.VMEM((tiles, rows, lanes), f32),
                 pltpu.VMEM((rows * tiles, lanes), f32),
             ],
-        )(here, line, kept, swapped)
+        )(*here, line, kept, swapped)
         sums = near_core(exchange(sums, CHAN))
-        return pl.pallas_call(
+        return run(
             last_kernel,
             out_shape=jax.ShapeDtypeStruct((own, n_y * width), bf16),
             scratch_shapes=[pltpu.VMEM((own, n_y * width), f32)],

time: 179 us -> 174 us (0.972)
  waiting for transfers between devices: 30.7 us -> 20.6 us
  starting transfers between devices: 78 us -> 86.7 us
  Pallas kernels: 12.1 us -> 8.38 us
  local copies, waits for them, and re-layouts: 0.05 us -> 2.38 us
    all_to_all x2, starting transfers between devices: 17.5 us -> 22.4 us  [exchange(): return lax.all_to_all(array, axes, 0, 0, tiled=True)]
    ppermute x1, waiting for transfers between devices: 4.85 us -> 0.01 us  [shards(): turned_weight = lax.ppermute(out_weight, FSDP + ('y',), turned())]
    ppermute x1 -> x2, waiting for transfers between devices: 8.46 us -> 3.84 us  [the longest x1 3.84 us: shards(): turned_far = lax.ppermute(turned_weight, 'zh', halves)]
    ppermute x1 -> x2, starting transfers between devices: 29.6 us -> 33.6 us  [the longest x1 17.8 us: shards(): turned_far = lax.ppermute(turned_weight, 'zh', halves)]
    pallas_call x9, Pallas kernels: 12.1 us -> 8.38 us  [the longest x1 2.06 us: shards(): run(local_kernel, out_shape=(near((rows, channels), f32), near((n_x * n_c...]
    unnamed x8 -> x11, local copies, waits for them, and re-layouts: 0.03 us -> 2.37 us
  transfers between devices with their start and end apart: 9 -> 10, of which waited for: 4 -> 3; matrix products, arithmetic and copies ran while one was open for 0% -> 1% of each run, Pallas kernels for 5% -> 4%
where the time goes in v3:
time: 174 us; the launch traced here: 173 us
  starting transfers between devices  86.7 us (50%)
  blocking collectives  54.2 us (31%)
  waiting for transfers between devices  20.6 us (12%)
  Pallas kernels  8.38 us (5%)
  local copies, waits for them, and re-layouts  2.38 us (1%)
    all_to_all x3, blocking collectives, exchange(): return lax.all_to_all(array, axes, 0, 0, tiled=True)  54.2 us
    all_to_all x2, starting transfers between devices, exchange(): return lax.all_to_all(array, axes, 0, 0, tiled=True)  22.4 us
    ppermute x1, starting transfers between devices, shards(): turned_far = lax.ppermute(turned_weight, 'zh', halves)  17.8 us
    all_to_all x2, waiting for transfers between devices, exchange(): return lax.all_to_all(array, axes, 0, 0, tiled=True)  16.7 us
    ppermute x1, starting transfers between devices, shards(): gate_far = lax.ppermute(gate_weight, 'zh', halves)  15.9 us
    ppermute x1, starting transfers between devices, shards(): half = near_core(lax.ppermute(half, 'zh', [(0, 1)]))  12.4 us
    ppermute x3, starting transfers between devices, shards(): lax.ppermute(mine, 'x', [(i, (i + back) % n_x) for i in range(n_x)])  10.9 us
    ppermute x1, starting transfers between devices, shards(): turned_weight = lax.ppermute(out_weight, FSDP + ('y',), turned())  5.41 us
  transfers between devices with their start and end apart: 10, of which 3 were waited for; matrix products, arithmetic and copies ran while one was open for 1% of the time, Pallas kernels for 4%

profile of v3, /device:TPU:6, one launch (start us, length us, event | category | flops | bytes accessed | tf_op | source)
XLA Modules:
  0.0 172.5 jit_solution(13703050447417813875)
XLA Ops:
  0.0 5.4 %collective-permute-start.1 = (bf16[256,128]{1,0:T(8,128)(2,1)}, bf16[256,128]{1,0:T(8,128)(2,1)S(1)}, u32[]{:S(2)}, u32[]{:S(2)}) collective-permute-start(bf16[256,128]{1,0:T(8,128)(2,1)} %param.19), channel_id=1, source_target_pairs={{0,0},{8,128},{16,256},{24,384},{32,512},{40,640},{48,768},{56,896... | collective-permute-start | bytes 196616 | tf_op jit(solution)/shard_map/ppermute | solution.py:230
  5.4 15.9 %collective-permute-start.2 = (bf16[256,128]{1,0:T(8,128)(2,1)}, bf16[256,128]{1,0:T(8,128)(2,1)S(1)}, u32[]{:S(2)}, u32[]{:S(2)}) collective-permute-start(bf16[256,128]{1,0:T(8,128)(2,1)} %param.13), channel_id=1, source_target_pairs={{0,512},{512,0},{1,513},{513,1},{2,514},{514,2},{3,515},{515,3},{4... | collective-permute-start | bytes 196616 | tf_op jit(solution)/shard_map/ppermute | solution.py:232
  21.3 0.9 constant_dynamic-update-slice_fusion.3
  22.1 0.0 collective-permute-done.1
  22.1 17.8 %collective-permute-start.3 = (bf16[256,128]{1,0:T(8,128)(2,1)S(1)}, bf16[256,128]{1,0:T(8,128)(2,1)S(1)}, u32[]{:S(2)}, u32[]{:S(2)}) collective-permute-start(bf16[256,128]{1,0:T(8,128)(2,1)S(1)} %collective-permute-done.1), channel_id=1, source_target_pairs={{0,512},{512,0},{1,513},{513,1},{2,514},{514,2},{3,515},{515,3},{4... | collective-permute-start | bytes 196616 | tf_op jit(solution)/shard_map/ppermute | solution.py:233
  40.0 3.8 %collective-permute-done.3 = bf16[256,128]{1,0:T(8,128)(2,1)S(1)} collective-permute-done((bf16[256,128]{1,0:T(8,128)(2,1)S(1)}, bf16[256,128]{1,0:T(8,128)(2,1)S(1)}, u32[]{:S(2)}, u32[]{:S(2)}) %collective-permute-start.3) | collective-permute-done | bytes 65568 | tf_op jit(solution)/shard_map/ppermute | solution.py:233
  43.8 4.1 %collective-permute-start.6 = (bf16[1024,128]{1,0:T(8,128)(2,1)S(1)}, bf16[1024,128]{1,0:T(8,128)(2,1)S(1)}, u32[]{:S(2)}, u32[]{:S(2)}) collective-permute-start(bf16[1024,128]{1,0:T(8,128)(2,1)S(1)} %constant_dynamic-update-slice_fusion), channel_id=1, source_target_pairs={{0,384},{128,0},{256,128},{384,256},{1,385},{129,1},{257,129},{385... | collective-permute-start | bytes 786440 | tf_op jit(solution)/shard_map/ppermute | solution.py:249
  47.9 3.7 %collective-permute-start.5 = (bf16[1024,128]{1,0:T(8,128)(2,1)S(1)}, bf16[1024,128]{1,0:T(8,128)(2,1)S(1)}, u32[]{:S(2)}, u32[]{:S(2)}) collective-permute-start(bf16[1024,128]{1,0:T(8,128)(2,1)S(1)} %constant_dynamic-update-slice_fusion), channel_id=1, source_target_pairs={{0,256},{128,384},{256,0},{384,128},{1,257},{129,385},{257,1},{385... | collective-permute-start | bytes 786440 | tf_op jit(solution)/shard_map/ppermute | solution.py:249
  51.6 3.1 %collective-permute-start.4 = (bf16[1024,128]{1,0:T(8,128)(2,1)S(1)}, bf16[1024,128]{1,0:T(8,128)(2,1)S(1)}, u32[]{:S(2)}, u32[]{:S(2)}) collective-permute-start(bf16[1024,128]{1,0:T(8,128)(2,1)S(1)} %constant_dynamic-update-slice_fusion), channel_id=1, source_target_pairs={{0,128},{128,256},{256,384},{384,0},{1,129},{129,257},{257,385},{3... | collective-permute-start | bytes 786440 | tf_op jit(solution)/shard_map/ppermute | solution.py:249
  54.8 1.7 %shard_map.100 = bf16[64,8,128]{2,1,0:T(8,128)(2,1)} custom-call(bf16[288,128]{1,0:T(8,128)(2,1)} %bitcast.27, bf16[128,128]{1,0:T(8,128)(2,1)} %conv.5), custom_call_target="tpu_custom_call" | custom-call | tf_op jit(solution)/shard_map/pallas_call | solution.py:237
  56.5 17.9 %all-to-all-start = ((bf16[64,8,128]{2,1,0:T(8,128)(2,1)}), bf16[64,8,128]{2,1,0:T(8,128)(2,1)S(1)}, u32[]{:S(2)}, u32[]{:S(2)}) async-start(bf16[64,8,128]{2,1,0:T(8,128)(2,1)} %shard_map.100), calls=%async_computation | async-start | bytes 262144 | tf_op jit(solution)/shard_map/all_to_all | solution.py:29
  74.5 0.1 pad_maximum_fusion.kept
  74.6 1.9 %collective-permute-start.7 = (bf16[4,1024,128]{2,1,0:T(8,128)(2,1)S(1)}, bf16[4,1024,128]{2,1,0:T(8,128)(2,1)S(1)}, u32[]{:S(2)}, u32[]{:S(2)}) collective-permute-start(bf16[4,1024,128]{2,1,0:T(8,128)(2,1)S(1)} %pad_maximum_fusion.kept), channel_id=1, source_target_pairs={{0,64},{64,0},{1,65},{65,1},{2,66},{66,2},{3,67},{67,3},{4,68},{68... | collective-permute-start | bytes 3145736 | tf_op jit(solution)/shard_map/ppermute | solution.py:251
  76.5 13.0 %all-to-all-done.shares = bf16[64,8,128]{2,1,0:T(8,128)(2,1)S(1)} async-done(((bf16[64,8,128]{2,1,0:T(8,128)(2,1)}), bf16[64,8,128]{2,1,0:T(8,128)(2,1)S(1)}, u32[]{:S(2)}, u32[]{:S(2)}) %all-to-all-start) | async-done | bytes 131104 | tf_op jit(solution)/shard_map/all_to_all | solution.py:29
  89.5 0.8 shard_map.101
  90.3 20.2 %all_to_all.25 = bf16[64,8,128]{2,1,0:T(8,128)(2,1)S(1)} all-to-all(bf16[64,8,128]{2,1,0:T(8,128)(2,1)} %shard_map.101), channel_id=1, replica_groups=mesh['zh'=2,'x'=4,'core'=2,'y'=8,'z'=8] {'y','z'}, dimensions={0} | all-to-all | bytes 262144 | tf_op jit(solution)/shard_map/all_to_all | solution.py:29
  110.5 2.1 %shard_map.102 = (f32[128,128]{1,0:T(8,128)S(1)}, f32[8,24,128]{2,1,0:T(8,128)}) custom-call(bf16[512,128]{1,0:T(8,128)(2,1)S(1)} %bitcast.15, bf16[128,128]{1,0:T(8,128)(2,1)} %conv.5, bf16[256,128]{1,0:T(8,128)(2,1)} %dt_weight.1, f32[1,128]{1,0:T(1,128)} %bitcast.28, f32[16,128]{1,0:T(8,128)} %bitcast.18), custom_call_target="tpu_custom_call" | custom-call | tf_op jit(solution)/shard_map/pallas_call | solution.py:256
  112.6 4.5 %all-to-all-start.2 = ((f32[8,24,128]{2,1,0:T(8,128)}), f32[8,24,128]{2,1,0:T(8,128)S(1)}, u32[]{:S(2)}, u32[]{:S(2)}) async-start(f32[8,24,128]{2,1,0:T(8,128)} %get-tuple-element.14), calls=%async_computation.2 | async-start | bytes 196608 | tf_op jit(solution)/shard_map/all_to_all | solution.py:29
  117.1 3.7 %all-to-all-done.2.gathered = f32[8,24,128]{2,1,0:T(8,128)S(1)} async-done(((f32[8,24,128]{2,1,0:T(8,128)}), f32[8,24,128]{2,1,0:T(8,128)S(1)}, u32[]{:S(2)}, u32[]{:S(2)}) %all-to-all-start.2) | async-done | bytes 98336 | tf_op jit(solution)/shard_map/all_to_all | solution.py:29
  120.8 0.1 shard_map.104
  120.9 12.4 %collective-permute-start = (f32[24,128]{1,0:T(8,128)S(1)}, f32[24,128]{1,0:T(8,128)S(1)}, u32[]{:S(2)}, u32[]{:S(2)}) collective-permute-start(f32[24,128]{1,0:T(8,128)S(1)} %get-tuple-element.15), channel_id=1, source_target_pairs={{0,512},{1,513},{2,514},{3,515},{4,516},{5,517},{6,518},{7,519},{8... | collective-permute-start | bytes 36872 | tf_op jit(solution)/shard_map/ppermute | solution.py:266
  133.3 1.6 shard_map.103
  135.0 0.0 copy-start
  135.0 1.2 copy-done
  136.2 0.4 shard_map.105.gate_pre
  136.6 0.2 copy-done.2
  136.9 0.0 copy-done.3
  136.9 0.5 shard_map.106
  137.4 14.1 %all_to_all.26.gated = bf16[8,128,128]{2,1,0:T(8,128)(2,1)S(1)} all-to-all(bf16[8,128,128]{2,1,0:T(8,128)(2,1)S(1)} %shard_map.106), channel_id=1, replica_groups=mesh['zh'=2,'x'=4,'core'=2,'y'=8,'z'=8] {'y'}, dimensions={0} | all-to-all | bytes 524288 | tf_op jit(solution)/shard_map/all_to_all | solution.py:29
  151.6 0.5 shard_map.107
  152.1 19.8 %all_to_all.27.shares = bf16[64,8,128]{2,1,0:T(8,128)(2,1)S(1)} all-to-all(bf16[64,8,128]{2,1,0:T(8,128)(2,1)S(1)} %shard_map.107), channel_id=1, replica_groups=mesh['zh'=2,'x'=4,'core'=2,'y'=8,'z'=8] {'y','z'}, dimensions={0} | all-to-all | bytes 262144 | tf_op jit(solution)/shard_map/all_to_all | solution.py:29
  171.9 0.7 shard_map.108
  (13 shorter events, 0.1 us)
Async XLA Ops:
  0.0 22.1 %collective-permute-start.1 = (bf16[256,128]{1,0:T(8,128)(2,1)}, bf16[256,128]{1,0:T(8,128)(2,1)S(1)}, u32[]{:S(2)}, u32[]{:S(2)}) collective-permute-start(bf16[256,128]{1,0:T(8,128)(2,1)} %param.19), channel_id=1, source_target_pairs={{0,0},{8,128},{16,256},{24,384},{32,512},{40,640},{48,768},{56,896... | collective-permute-start | bytes 196616 | tf_op jit(solution)/shard_map/ppermute | solution.py:230
  5.4 34.5 %collective-permute-start.2 = (bf16[256,128]{1,0:T(8,128)(2,1)}, bf16[256,128]{1,0:T(8,128)(2,1)S(1)}, u32[]{:S(2)}, u32[]{:S(2)}) collective-permute-start(bf16[256,128]{1,0:T(8,128)(2,1)} %param.13), channel_id=1, source_target_pairs={{0,512},{512,0},{1,513},{513,1},{2,514},{514,2},{3,515},{515,3},{4... | collective-permute-start | bytes 196616 | tf_op jit(solution)/shard_map/ppermute | solution.py:232
  22.1 21.7 %collective-permute-start.3 = (bf16[256,128]{1,0:T(8,128)(2,1)S(1)}, bf16[256,128]{1,0:T(8,128)(2,1)S(1)}, u32[]{:S(2)}, u32[]{:S(2)}) collective-permute-start(bf16[256,128]{1,0:T(8,128)(2,1)S(1)} %collective-permute-done.1), channel_id=1, source_target_pairs={{0,512},{512,0},{1,513},{513,1},{2,514},{514,2},{3,515},{515,3},{4... | collective-permute-start | bytes 196616 | tf_op jit(solution)/shard_map/ppermute | solution.py:233
  43.8 30.6 %collective-permute-start.6 = (bf16[1024,128]{1,0:T(8,128)(2,1)S(1)}, bf16[1024,128]{1,0:T(8,128)(2,1)S(1)}, u32[]{:S(2)}, u32[]{:S(2)}) collective-permute-start(bf16[1024,128]{1,0:T(8,128)(2,1)S(1)} %constant_dynamic-update-slice_fusion), channel_id=1, source_target_pairs={{0,384},{128,0},{256,128},{384,256},{1,385},{129,1},{257,129},{385... | collective-permute-start | bytes 786440 | tf_op jit(solution)/shard_map/ppermute | solution.py:249
  47.9 26.5 %collective-permute-start.5 = (bf16[1024,128]{1,0:T(8,128)(2,1)S(1)}, bf16[1024,128]{1,0:T(8,128)(2,1)S(1)}, u32[]{:S(2)}, u32[]{:S(2)}) collective-permute-start(bf16[1024,128]{1,0:T(8,128)(2,1)S(1)} %constant_dynamic-update-slice_fusion), channel_id=1, source_target_pairs={{0,256},{128,384},{256,0},{384,128},{1,257},{129,385},{257,1},{385... | collective-permute-start | bytes 786440 | tf_op jit(solution)/shard_map/ppermute | solution.py:249
  51.6 22.8 %collective-permute-start.4 = (bf16[1024,128]{1,0:T(8,128)(2,1)S(1)}, bf16[1024,128]{1,0:T(8,128)(2,1)S(1)}, u32[]{:S(2)}, u32[]{:S(2)}) collective-permute-start(bf16[1024,128]{1,0:T(8,128)(2,1)S(1)} %constant_dynamic-update-slice_fusion), channel_id=1, source_target_pairs={{0,128},{128,256},{256,384},{384,0},{1,129},{129,257},{257,385},{3... | collective-permute-start | bytes 786440 | tf_op jit(solution)/shard_map/ppermute | solution.py:249
  56.5 33.1 %all-to-all-start = ((bf16[64,8,128]{2,1,0:T(8,128)(2,1)}), bf16[64,8,128]{2,1,0:T(8,128)(2,1)S(1)}, u32[]{:S(2)}, u32[]{:S(2)}) async-start(bf16[64,8,128]{2,1,0:T(8,128)(2,1)} %shard_map.100), calls=%async_computation | async-start | bytes 262144 | tf_op jit(solution)/shard_map/all_to_all | solution.py:29
  74.6 60.3 %collective-permute-start.7 = (bf16[4,1024,128]{2,1,0:T(8,128)(2,1)S(1)}, bf16[4,1024,128]{2,1,0:T(8,128)(2,1)S(1)}, u32[]{:S(2)}, u32[]{:S(2)}) collective-permute-start(bf16[4,1024,128]{2,1,0:T(8,128)(2,1)S(1)} %pad_maximum_fusion.kept), channel_id=1, source_target_pairs={{0,64},{64,0},{1,65},{65,1},{2,66},{66,2},{3,67},{67,3},{4,68},{68... | collective-permute-start | bytes 3145736 | tf_op jit(solution)/shard_map/ppermute | solution.py:251
  112.6 8.2 %all-to-all-start.2 = ((f32[8,24,128]{2,1,0:T(8,128)}), f32[8,24,128]{2,1,0:T(8,128)S(1)}, u32[]{:S(2)}, u32[]{:S(2)}) async-start(f32[8,24,128]{2,1,0:T(8,128)} %get-tuple-element.14), calls=%async_computation.2 | async-start | bytes 196608 | tf_op jit(solution)/shard_map/all_to_all | solution.py:29
  117.1 3.7 %copy-start.1 = (f32[128,16]{0,1:T(8,128)S(1)}, f32[128,16]{0,1:T(8,128)}, u32[]{:S(2)}) copy-start(f32[128,16]{0,1:T(8,128)} %param.17) | copy-start | bytes 24580
  120.9 15.7 %collective-permute-start = (f32[24,128]{1,0:T(8,128)S(1)}, f32[24,128]{1,0:T(8,128)S(1)}, u32[]{:S(2)}, u32[]{:S(2)}) collective-permute-start(f32[24,128]{1,0:T(8,128)S(1)} %get-tuple-element.15), channel_id=1, source_target_pairs={{0,512},{1,513},{2,514},{3,515},{4,516},{5,517},{6,518},{7,519},{8... | collective-permute-start | bytes 36872 | tf_op jit(solution)/shard_map/ppermute | solution.py:266
  135.0 1.2 copy-start
  136.2 0.7 copy-start.2
  136.2 0.7 copy-start.3

commit v4 on v3

--- a/solution.py
+++ b/solution.py
@@ -228,9 +228,8 @@
         shape, near = jax.ShapeDtypeStruct, pltpu.VMEM
 
         turned_weight = lax.ppermute(out_weight, FSDP + ("y",), turned())
-        halves = [(0, 1), (1, 0)]
-        gate_far = lax.ppermute(gate_weight, "zh", halves)
-        turned_far = lax.ppermute(turned_weight, "zh", halves)
+        pair = jnp.concatenate([gate_weight, turned_weight], axis=0)
+        far = lax.ppermute(pair, "zh", [(0, 1), (1, 0)])
 
         used = xproj_weight.shape[1] + 2 * STATE
         piece = -(-used // (8 * n_c)) * 8
@@ -243,7 +242,7 @@
         )(own_piece, near_core(shares))
         proj = exchange(summed, CHAN).reshape(n_c * piece, rows)
 
-        mine = jnp.concatenate([gate_weight, turned_weight, gate_far, turned_far], axis=0)
+        mine = jnp.concatenate([pair, far], axis=0)
         kept = [mine]
         for back in range(1, n_x):
             kept.append(lax.ppermute(mine, "x", [(i, (i + back) % n_x) for i in range(n_x)]))

time: 174 us -> 176 us (1.011)
  waiting for transfers between devices: 20.6 us -> 30.7 us
  starting transfers between devices: 86.7 us -> 78 us
    all_to_all x2, starting transfers between devices: 22.4 us -> 17.5 us  [exchange(): return lax.all_to_all(array, axes, 0, 0, tiled=True)]
    ppermute x1, waiting for transfers between devices: 0.01 us -> 4.85 us  [shards(): turned_weight = lax.ppermute(out_weight, FSDP + ('y',), turned())]
    ppermute x2 -> x1, waiting for transfers between devices: 3.84 us -> 8.46 us  [shards(): far = lax.ppermute(pair, 'zh', [(0, 1), (1, 0)])]
    ppermute x2 -> x1, starting transfers between devices: 33.6 us -> 29.6 us  [shards(): far = lax.ppermute(pair, 'zh', [(0, 1), (1, 0)])]
  transfers between devices with their start and end apart: 10 -> 9, of which waited for: 3 -> 4; matrix products, arithmetic and copies ran while one was open for 1% -> 0% of each run, Pallas kernels for 4% -> 4%
where the time goes in v4:
time: 176 us; the launch traced here: 174 us
  starting transfers between devices  78 us (44%)
  blocking collectives  54.5 us (31%)
  waiting for transfers between devices  30.7 us (17%)
  Pallas kernels  8.37 us (5%)
    all_to_all x3, blocking collectives, exchange(): return lax.all_to_all(array, axes, 0, 0, tiled=True)  54.5 us
    ppermute x1, starting transfers between devices, shards(): far = lax.ppermute(pair, 'zh', [(0, 1), (1, 0)])  29.6 us
    all_to_all x2, starting transfers between devices, exchange(): return lax.all_to_all(array, axes, 0, 0, tiled=True)  17.5 us
    all_to_all x2, waiting for transfers between devices, exchange(): return lax.all_to_all(array, axes, 0, 0, tiled=True)  17.4 us
    ppermute x3, starting transfers between devices, shards(): lax.ppermute(mine, 'x', [(i, (i + back) % n_x) for i in range(n_x)])  11.7 us
    ppermute x1, starting transfers between devices, shards(): half = near_core(lax.ppermute(half, 'zh', [(0, 1)]))  11.7 us
    ppermute x1, waiting for transfers between devices, shards(): far = lax.ppermute(pair, 'zh', [(0, 1), (1, 0)])  8.46 us
    ppermute x1, starting transfers between devices, shards(): turned_weight = lax.ppermute(out_weight, FSDP + ('y',), turned())  5.54 us
  transfers between devices with their start and end apart: 9, of which 4 were waited for; matrix products, arithmetic and copies ran while one was open for 0% of the time, Pallas kernels for 4%

profile of v4, /device:TPU:6, one launch (start us, length us, event | category | flops | bytes accessed | tf_op | source)
XLA Modules:
  0.0 174.3 jit_solution(8297448541186498485)
XLA Ops:
  0.0 5.5 %collective-permute-start.1 = (bf16[256,128]{1,0:T(8,128)(2,1)}, bf16[256,128]{1,0:T(8,128)(2,1)S(1)}, u32[]{:S(2)}, u32[]{:S(2)}) collective-permute-start(bf16[256,128]{1,0:T(8,128)(2,1)} %param.19), channel_id=1, source_target_pairs={{0,0},{8,128},{16,256},{24,384},{32,512},{40,640},{48,768},{56,896... | collective-permute-start | bytes 196616 | tf_op jit(solution)/shard_map/ppermute | solution.py:230
  5.6 4.8 %collective-permute-done.1 = bf16[256,128]{1,0:T(8,128)(2,1)S(1)} collective-permute-done((bf16[256,128]{1,0:T(8,128)(2,1)}, bf16[256,128]{1,0:T(8,128)(2,1)S(1)}, u32[]{:S(2)}, u32[]{:S(2)}) %collective-permute-start.1) | collective-permute-done | bytes 65568 | tf_op jit(solution)/shard_map/ppermute | solution.py:230
  10.4 0.8 pad_maximum_fusion.1
  11.3 29.6 %collective-permute-start.2 = (bf16[512,128]{1,0:T(8,128)(2,1)S(1)}, bf16[512,128]{1,0:T(8,128)(2,1)S(1)}, u32[]{:S(2)}, u32[]{:S(2)}) collective-permute-start(bf16[512,128]{1,0:T(8,128)(2,1)S(1)} %pad_maximum_fusion.1), channel_id=1, source_target_pairs={{0,512},{512,0},{1,513},{513,1},{2,514},{514,2},{3,515},{515,3},{4... | collective-permute-start | bytes 393224 | tf_op jit(solution)/shard_map/ppermute | solution.py:232
  41.0 8.5 %collective-permute-done.2 = bf16[512,128]{1,0:T(8,128)(2,1)S(1)} collective-permute-done((bf16[512,128]{1,0:T(8,128)(2,1)S(1)}, bf16[512,128]{1,0:T(8,128)(2,1)S(1)}, u32[]{:S(2)}, u32[]{:S(2)}) %collective-permute-start.2) | collective-permute-done | bytes 131104 | tf_op jit(solution)/shard_map/ppermute | solution.py:232
  49.4 5.2 %collective-permute-start.5 = (bf16[1024,128]{1,0:T(8,128)(2,1)S(1)}, bf16[1024,128]{1,0:T(8,128)(2,1)S(1)}, u32[]{:S(2)}, u32[]{:S(2)}) collective-permute-start(bf16[1024,128]{1,0:T(8,128)(2,1)S(1)} %constant_dynamic-update-slice_fusion), channel_id=1, source_target_pairs={{0,384},{128,0},{256,128},{384,256},{1,385},{129,1},{257,129},{385... | collective-permute-start | bytes 786440 | tf_op jit(solution)/shard_map/ppermute | solution.py:248
  54.7 2.2 %collective-permute-start.4 = (bf16[1024,128]{1,0:T(8,128)(2,1)S(1)}, bf16[1024,128]{1,0:T(8,128)(2,1)S(1)}, u32[]{:S(2)}, u32[]{:S(2)}) collective-permute-start(bf16[1024,128]{1,0:T(8,128)(2,1)S(1)} %constant_dynamic-update-slice_fusion), channel_id=1, source_target_pairs={{0,256},{128,384},{256,0},{384,128},{1,257},{129,385},{257,1},{385... | collective-permute-start | bytes 786440 | tf_op jit(solution)/shard_map/ppermute | solution.py:248
  56.9 4.3 %collective-permute-start.3 = (bf16[1024,128]{1,0:T(8,128)(2,1)S(1)}, bf16[1024,128]{1,0:T(8,128)(2,1)S(1)}, u32[]{:S(2)}, u32[]{:S(2)}) collective-permute-start(bf16[1024,128]{1,0:T(8,128)(2,1)S(1)} %constant_dynamic-update-slice_fusion), channel_id=1, source_target_pairs={{0,128},{128,256},{256,384},{384,0},{1,129},{129,257},{257,385},{3... | collective-permute-start | bytes 786440 | tf_op jit(solution)/shard_map/ppermute | solution.py:248
  61.2 1.7 shard_map.100
  62.9 13.0 %all-to-all-start = ((bf16[64,8,128]{2,1,0:T(8,128)(2,1)}), bf16[64,8,128]{2,1,0:T(8,128)(2,1)S(1)}, u32[]{:S(2)}, u32[]{:S(2)}) async-start(bf16[64,8,128]{2,1,0:T(8,128)(2,1)} %shard_map.100), calls=%async_computation | async-start | bytes 262144 | tf_op jit(solution)/shard_map/all_to_all | solution.py:29
  75.9 0.0 collective-permute-done.5
  75.9 0.1 pad_maximum_fusion.kept
  76.1 1.9 %collective-permute-start.6 = (bf16[4,1024,128]{2,1,0:T(8,128)(2,1)S(1)}, bf16[4,1024,128]{2,1,0:T(8,128)(2,1)S(1)}, u32[]{:S(2)}, u32[]{:S(2)}) collective-permute-start(bf16[4,1024,128]{2,1,0:T(8,128)(2,1)S(1)} %pad_maximum_fusion.kept), channel_id=1, source_target_pairs={{0,64},{64,0},{1,65},{65,1},{2,66},{66,2},{3,67},{67,3},{4,68},{68... | collective-permute-start | bytes 3145736 | tf_op jit(solution)/shard_map/ppermute | solution.py:250
  78.0 13.7 %all-to-all-done.shares = bf16[64,8,128]{2,1,0:T(8,128)(2,1)S(1)} async-done(((bf16[64,8,128]{2,1,0:T(8,128)(2,1)}), bf16[64,8,128]{2,1,0:T(8,128)(2,1)S(1)}, u32[]{:S(2)}, u32[]{:S(2)}) %all-to-all-start) | async-done | bytes 131104 | tf_op jit(solution)/shard_map/all_to_all | solution.py:29
  91.7 0.8 shard_map.101
  92.4 20.8 %all_to_all.25 = bf16[64,8,128]{2,1,0:T(8,128)(2,1)S(1)} all-to-all(bf16[64,8,128]{2,1,0:T(8,128)(2,1)} %shard_map.101), channel_id=1, replica_groups=mesh['zh'=2,'x'=4,'core'=2,'y'=8,'z'=8] {'y','z'}, dimensions={0} | all-to-all | bytes 262144 | tf_op jit(solution)/shard_map/all_to_all | solution.py:29
  113.3 2.1 %shard_map.102 = (f32[128,128]{1,0:T(8,128)S(1)}, f32[8,24,128]{2,1,0:T(8,128)}) custom-call(bf16[512,128]{1,0:T(8,128)(2,1)S(1)} %bitcast.15, bf16[128,128]{1,0:T(8,128)(2,1)} %conv.5, bf16[256,128]{1,0:T(8,128)(2,1)} %dt_weight.1, f32[1,128]{1,0:T(1,128)} %bitcast.28, f32[16,128]{1,0:T(8,128)} %bitcast.18), custom_call_target="tpu_custom_call" | custom-call | tf_op jit(solution)/shard_map/pallas_call | solution.py:255
  115.4 4.5 %all-to-all-start.2 = ((f32[8,24,128]{2,1,0:T(8,128)}), f32[8,24,128]{2,1,0:T(8,128)S(1)}, u32[]{:S(2)}, u32[]{:S(2)}) async-start(f32[8,24,128]{2,1,0:T(8,128)} %get-tuple-element.14), calls=%async_computation.2 | async-start | bytes 196608 | tf_op jit(solution)/shard_map/all_to_all | solution.py:29
  119.9 3.7 %all-to-all-done.2.gathered = f32[8,24,128]{2,1,0:T(8,128)S(1)} async-done(((f32[8,24,128]{2,1,0:T(8,128)}), f32[8,24,128]{2,1,0:T(8,128)S(1)}, u32[]{:S(2)}, u32[]{:S(2)}) %all-to-all-start.2) | async-done | bytes 98336 | tf_op jit(solution)/shard_map/all_to_all | solution.py:29
  123.6 0.1 shard_map.104
  123.7 11.7 %collective-permute-start = (f32[24,128]{1,0:T(8,128)S(1)}, f32[24,128]{1,0:T(8,128)S(1)}, u32[]{:S(2)}, u32[]{:S(2)}) collective-permute-start(f32[24,128]{1,0:T(8,128)S(1)} %get-tuple-element.15), channel_id=1, source_target_pairs={{0,512},{1,513},{2,514},{3,515},{4,516},{5,517},{6,518},{7,519},{8... | collective-permute-start | bytes 36872 | tf_op jit(solution)/shard_map/ppermute | solution.py:265
  135.4 1.6 shard_map.103
  137.0 0.0 copy-start
  137.0 1.2 copy-done
  138.2 0.4 shard_map.105.gate_pre
  138.7 0.2 copy-done.2
  138.9 0.0 copy-done.3
  138.9 0.5 shard_map.106
  139.5 14.1 %all_to_all.26.gated = bf16[8,128,128]{2,1,0:T(8,128)(2,1)S(1)} all-to-all(bf16[8,128,128]{2,1,0:T(8,128)(2,1)S(1)} %shard_map.106), channel_id=1, replica_groups=mesh['zh'=2,'x'=4,'core'=2,'y'=8,'z'=8] {'y'}, dimensions={0} | all-to-all | bytes 524288 | tf_op jit(solution)/shard_map/all_to_all | solution.py:29
  153.6 0.5 shard_map.107
  154.1 19.5 %all_to_all.27.shares = bf16[64,8,128]{2,1,0:T(8,128)(2,1)S(1)} all-to-all(bf16[64,8,128]{2,1,0:T(8,128)(2,1)S(1)} %shard_map.107), channel_id=1, replica_groups=mesh['zh'=2,'x'=4,'core'=2,'y'=8,'z'=8] {'y','z'}, dimensions={0} | all-to-all | bytes 262144 | tf_op jit(solution)/shard_map/all_to_all | solution.py:29
  173.6 0.7 shard_map.108
  (13 shorter events, 0.1 us)
Async XLA Ops:
  0.0 40.9 %copy-start.4 = (bf16[256,128]{1,0:T(8,128)(2,1)S(1)}, bf16[256,128]{1,0:T(8,128)(2,1)}, u32[]{:S(2)}) copy-start(bf16[256,128]{1,0:T(8,128)(2,1)} %param.13) | copy-start | bytes 196612
  0.0 10.4 %collective-permute-start.1 = (bf16[256,128]{1,0:T(8,128)(2,1)}, bf16[256,128]{1,0:T(8,128)(2,1)S(1)}, u32[]{:S(2)}, u32[]{:S(2)}) collective-permute-start(bf16[256,128]{1,0:T(8,128)(2,1)} %param.19), channel_id=1, source_target_pairs={{0,0},{8,128},{16,256},{24,384},{32,512},{40,640},{48,768},{56,896... | collective-permute-start | bytes 196616 | tf_op jit(solution)/shard_map/ppermute | solution.py:230
  11.3 38.2 %collective-permute-start.2 = (bf16[512,128]{1,0:T(8,128)(2,1)S(1)}, bf16[512,128]{1,0:T(8,128)(2,1)S(1)}, u32[]{:S(2)}, u32[]{:S(2)}) collective-permute-start(bf16[512,128]{1,0:T(8,128)(2,1)S(1)} %pad_maximum_fusion.1), channel_id=1, source_target_pairs={{0,512},{512,0},{1,513},{513,1},{2,514},{514,2},{3,515},{515,3},{4... | collective-permute-start | bytes 393224 | tf_op jit(solution)/shard_map/ppermute | solution.py:232
  49.4 26.5 %collective-permute-start.5 = (bf16[1024,128]{1,0:T(8,128)(2,1)S(1)}, bf16[1024,128]{1,0:T(8,128)(2,1)S(1)}, u32[]{:S(2)}, u32[]{:S(2)}) collective-permute-start(bf16[1024,128]{1,0:T(8,128)(2,1)S(1)} %constant_dynamic-update-slice_fusion), channel_id=1, source_target_pairs={{0,384},{128,0},{256,128},{384,256},{1,385},{129,1},{257,129},{385... | collective-permute-start | bytes 786440 | tf_op jit(solution)/shard_map/ppermute | solution.py:248
  54.7 21.2 %collective-permute-start.4 = (bf16[1024,128]{1,0:T(8,128)(2,1)S(1)}, bf16[1024,128]{1,0:T(8,128)(2,1)S(1)}, u32[]{:S(2)}, u32[]{:S(2)}) collective-permute-start(bf16[1024,128]{1,0:T(8,128)(2,1)S(1)} %constant_dynamic-update-slice_fusion), channel_id=1, source_target_pairs={{0,256},{128,384},{256,0},{384,128},{1,257},{129,385},{257,1},{385... | collective-permute-start | bytes 786440 | tf_op jit(solution)/shard_map/ppermute | solution.py:248
  56.9 19.0 %collective-permute-start.3 = (bf16[1024,128]{1,0:T(8,128)(2,1)S(1)}, bf16[1024,128]{1,0:T(8,128)(2,1)S(1)}, u32[]{:S(2)}, u32[]{:S(2)}) collective-permute-start(bf16[1024,128]{1,0:T(8,128)(2,1)S(1)} %constant_dynamic-update-slice_fusion), channel_id=1, source_target_pairs={{0,128},{128,256},{256,384},{384,0},{1,129},{129,257},{257,385},{3... | collective-permute-start | bytes 786440 | tf_op jit(solution)/shard_map/ppermute | solution.py:248
  62.9 28.8 %all-to-all-start = ((bf16[64,8,128]{2,1,0:T(8,128)(2,1)}), bf16[64,8,128]{2,1,0:T(8,128)(2,1)S(1)}, u32[]{:S(2)}, u32[]{:S(2)}) async-start(bf16[64,8,128]{2,1,0:T(8,128)(2,1)} %shard_map.100), calls=%async_computation | async-start | bytes 262144 | tf_op jit(solution)/shard_map/all_to_all | solution.py:29
  76.1 60.9 %collective-permute-start.6 = (bf16[4,1024,128]{2,1,0:T(8,128)(2,1)S(1)}, bf16[4,1024,128]{2,1,0:T(8,128)(2,1)S(1)}, u32[]{:S(2)}, u32[]{:S(2)}) collective-permute-start(bf16[4,1024,128]{2,1,0:T(8,128)(2,1)S(1)} %pad_maximum_fusion.kept), channel_id=1, source_target_pairs={{0,64},{64,0},{1,65},{65,1},{2,66},{66,2},{3,67},{67,3},{4,68},{68... | collective-permute-start | bytes 3145736 | tf_op jit(solution)/shard_map/ppermute | solution.py:250
  115.4 8.2 %all-to-all-start.2 = ((f32[8,24,128]{2,1,0:T(8,128)}), f32[8,24,128]{2,1,0:T(8,128)S(1)}, u32[]{:S(2)}, u32[]{:S(2)}) async-start(f32[8,24,128]{2,1,0:T(8,128)} %get-tuple-element.14), calls=%async_computation.2 | async-start | bytes 196608 | tf_op jit(solution)/shard_map/all_to_all | solution.py:29
  119.9 3.7 %copy-start.1 = (f32[128,16]{0,1:T(8,128)S(1)}, f32[128,16]{0,1:T(8,128)}, u32[]{:S(2)}) copy-start(f32[128,16]{0,1:T(8,128)} %param.17) | copy-start | bytes 24580
  123.7 15.0 %collective-permute-start = (f32[24,128]{1,0:T(8,128)S(1)}, f32[24,128]{1,0:T(8,128)S(1)}, u32[]{:S(2)}, u32[]{:S(2)}) collective-permute-start(f32[24,128]{1,0:T(8,128)S(1)} %get-tuple-element.15), channel_id=1, source_target_pairs={{0,512},{1,513},{2,514},{3,515},{4,516},{5,517},{6,518},{7,519},{8... | collective-permute-start | bytes 36872 | tf_op jit(solution)/shard_map/ppermute | solution.py:265
  137.0 1.2 copy-start
  138.2 0.7 copy-start.2
  138.2 0.7 copy-start.3

commit v5 on v4

--- a/solution.py
+++ b/solution.py
@@ -104,7 +104,17 @@
     all_out[STATE:] = jnp.broadcast_to(total, (rest, total.shape[1]))
 
 
-def gate_kernel(zh, x, core, hidden, kept, swapped, out):
+def gate_kernel(zh, x, core, far_hidden, kept, swapped, out, hidden, done):
+    parts = done.shape[0]
+    height = hidden.shape[0] // parts
+    fetches = []
+    for part in range(parts):
+        rows = pl.ds(part * height, height)
+        fetches.append(pltpu.make_async_copy(far_hidden.at[rows], hidden.at[rows], done.at[part]))
+    for fetch in fetches:
+        fetch.start()
+    for fetch in fetches:
+        fetch.wait()
     n_x, depth, _ = kept.shape
     block = depth // 4
     total = jnp.zeros(out.shape, jnp.float32)
@@ -267,8 +277,11 @@
             scan_kernel, out_shape=(near((rows, channels), f32),) * 2
         )(near_core(step), proj, conv_near, log_rate, skip_gain[None])
         gate_pre = run(
-            gate_kernel, in_specs=[SMEM] * 3 + [VMEM] * 3, out_shape=near((rows, channels), f32)
-        )(*here, hidden, kept, swapped)
+            gate_kernel,
+            in_specs=[SMEM] * 3 + [pl.BlockSpec(memory_space=pltpu.HBM)] + [VMEM] * 2,
+            out_shape=near((rows, channels), f32),
+            scratch_shapes=[pltpu.VMEM(hidden.shape, bf16), pltpu.SemaphoreType.DMA((4,))],
+        )(*here, pltpu.with_memory_space_constraint(hidden, pltpu.HBM), kept, swapped)
         gated = run(
             gated_kernel,
             out_shape=near((n_y, rows, channels), bf16),

time: 176 us -> 176 us (level)
  transfers between devices with their start and end apart: 9 -> 9, of which waited for: 4 -> 4; matrix products, arithmetic and copies ran while one was open for 0% -> 0% of each run, Pallas kernels for 4% -> 5%
where the time goes in v5:
time: 176 us; the launch traced here: 174 us
  starting transfers between devices  78 us (44%)
  blocking collectives  54.5 us (31%)
  waiting for transfers between devices  30.7 us (17%)
  Pallas kernels  9.58 us (5%)
    all_to_all x3, blocking collectives, exchange(): return lax.all_to_all(array, axes, 0, 0, tiled=True)  54.5 us
    ppermute x1, starting transfers between devices, shards(): far = lax.ppermute(pair, 'zh', [(0, 1), (1, 0)])  29.6 us
    all_to_all x2, starting transfers between devices, exchange(): return lax.all_to_all(array, axes, 0, 0, tiled=True)  17.5 us
    all_to_all x2, waiting for transfers between devices, exchange(): return lax.all_to_all(array, axes, 0, 0, tiled=True)  17.4 us
    ppermute x3, starting transfers between devices, shards(): lax.ppermute(mine, 'x', [(i, (i + back) % n_x) for i in range(n_x)])  11.7 us
    ppermute x1, starting transfers between devices, shards(): half = near_core(lax.ppermute(half, 'zh', [(0, 1)]))  11.7 us
    ppermute x1, waiting for transfers between devices, shards(): far = lax.ppermute(pair, 'zh', [(0, 1), (1, 0)])  8.46 us
    ppermute x1, starting transfers between devices, shards(): turned_weight = lax.ppermute(out_weight, FSDP + ('y',), turned())  5.54 us
  transfers between devices with their start and end apart: 9, of which 4 were waited for; matrix products, arithmetic and copies ran while one was open for 0% of the time, Pallas kernels for 5%

profile of v5, /device:TPU:6, one launch (start us, length us, event | category | flops | bytes accessed | tf_op | source)
XLA Modules:
  0.0 174.0 jit_solution(9618105155827486039)
XLA Ops:
  0.0 5.5 %collective-permute-start.1 = (bf16[256,128]{1,0:T(8,128)(2,1)}, bf16[256,128]{1,0:T(8,128)(2,1)S(1)}, u32[]{:S(2)}, u32[]{:S(2)}) collective-permute-start(bf16[256,128]{1,0:T(8,128)(2,1)} %param.19), channel_id=1, source_target_pairs={{0,0},{8,128},{16,256},{24,384},{32,512},{40,640},{48,768},{56,896... | collective-permute-start | bytes 196616 | tf_op jit(solution)/shard_map/ppermute | solution.py:240
  5.6 4.8 %collective-permute-done.1 = bf16[256,128]{1,0:T(8,128)(2,1)S(1)} collective-permute-done((bf16[256,128]{1,0:T(8,128)(2,1)}, bf16[256,128]{1,0:T(8,128)(2,1)S(1)}, u32[]{:S(2)}, u32[]{:S(2)}) %collective-permute-start.1) | collective-permute-done | bytes 65568 | tf_op jit(solution)/shard_map/ppermute | solution.py:240
  10.4 0.8 pad_maximum_fusion.1
  11.3 29.6 %collective-permute-start.2 = (bf16[512,128]{1,0:T(8,128)(2,1)S(1)}, bf16[512,128]{1,0:T(8,128)(2,1)S(1)}, u32[]{:S(2)}, u32[]{:S(2)}) collective-permute-start(bf16[512,128]{1,0:T(8,128)(2,1)S(1)} %pad_maximum_fusion.1), channel_id=1, source_target_pairs={{0,512},{512,0},{1,513},{513,1},{2,514},{514,2},{3,515},{515,3},{4... | collective-permute-start | bytes 393224 | tf_op jit(solution)/shard_map/ppermute | solution.py:242
  41.0 8.5 %collective-permute-done.2 = bf16[512,128]{1,0:T(8,128)(2,1)S(1)} collective-permute-done((bf16[512,128]{1,0:T(8,128)(2,1)S(1)}, bf16[512,128]{1,0:T(8,128)(2,1)S(1)}, u32[]{:S(2)}, u32[]{:S(2)}) %collective-permute-start.2) | collective-permute-done | bytes 131104 | tf_op jit(solution)/shard_map/ppermute | solution.py:242
  49.4 5.2 %collective-permute-start.5 = (bf16[1024,128]{1,0:T(8,128)(2,1)S(1)}, bf16[1024,128]{1,0:T(8,128)(2,1)S(1)}, u32[]{:S(2)}, u32[]{:S(2)}) collective-permute-start(bf16[1024,128]{1,0:T(8,128)(2,1)S(1)} %constant_dynamic-update-slice_fusion), channel_id=1, source_target_pairs={{0,384},{128,0},{256,128},{384,256},{1,385},{129,1},{257,129},{385... | collective-permute-start | bytes 786440 | tf_op jit(solution)/shard_map/ppermute | solution.py:258
  54.7 2.2 %collective-permute-start.4 = (bf16[1024,128]{1,0:T(8,128)(2,1)S(1)}, bf16[1024,128]{1,0:T(8,128)(2,1)S(1)}, u32[]{:S(2)}, u32[]{:S(2)}) collective-permute-start(bf16[1024,128]{1,0:T(8,128)(2,1)S(1)} %constant_dynamic-update-slice_fusion), channel_id=1, source_target_pairs={{0,256},{128,384},{256,0},{384,128},{1,257},{129,385},{257,1},{385... | collective-permute-start | bytes 786440 | tf_op jit(solution)/shard_map/ppermute | solution.py:258
  56.9 4.3 %collective-permute-start.3 = (bf16[1024,128]{1,0:T(8,128)(2,1)S(1)}, bf16[1024,128]{1,0:T(8,128)(2,1)S(1)}, u32[]{:S(2)}, u32[]{:S(2)}) collective-permute-start(bf16[1024,128]{1,0:T(8,128)(2,1)S(1)} %constant_dynamic-update-slice_fusion), channel_id=1, source_target_pairs={{0,128},{128,256},{256,384},{384,0},{1,129},{129,257},{257,385},{3... | collective-permute-start | bytes 786440 | tf_op jit(solution)/shard_map/ppermute | solution.py:258
  61.2 1.7 shard_map.100
  62.9 13.0 %all-to-all-start = ((bf16[64,8,128]{2,1,0:T(8,128)(2,1)}), bf16[64,8,128]{2,1,0:T(8,128)(2,1)S(1)}, u32[]{:S(2)}, u32[]{:S(2)}) async-start(bf16[64,8,128]{2,1,0:T(8,128)(2,1)} %shard_map.100), calls=%async_computation | async-start | bytes 262144 | tf_op jit(solution)/shard_map/all_to_all | solution.py:29
  75.9 0.0 collective-permute-done.5
  75.9 0.0 collective-permute-done.3
  75.9 0.1 pad_maximum_fusion.kept
  76.1 1.9 %collective-permute-start.6 = (bf16[4,1024,128]{2,1,0:T(8,128)(2,1)S(1)}, bf16[4,1024,128]{2,1,0:T(8,128)(2,1)S(1)}, u32[]{:S(2)}, u32[]{:S(2)}) collective-permute-start(bf16[4,1024,128]{2,1,0:T(8,128)(2,1)S(1)} %pad_maximum_fusion.kept), channel_id=1, source_target_pairs={{0,64},{64,0},{1,65},{65,1},{2,66},{66,2},{3,67},{67,3},{4,68},{68... | collective-permute-start | bytes 3145736 | tf_op jit(solution)/shard_map/ppermute | solution.py:260
  78.0 13.7 %all-to-all-done.shares = bf16[64,8,128]{2,1,0:T(8,128)(2,1)S(1)} async-done(((bf16[64,8,128]{2,1,0:T(8,128)(2,1)}), bf16[64,8,128]{2,1,0:T(8,128)(2,1)S(1)}, u32[]{:S(2)}, u32[]{:S(2)}) %all-to-all-start) | async-done | bytes 131104 | tf_op jit(solution)/shard_map/all_to_all | solution.py:29
  91.7 0.7 shard_map.101
  92.4 20.8 %all_to_all.25 = bf16[64,8,128]{2,1,0:T(8,128)(2,1)S(1)} all-to-all(bf16[64,8,128]{2,1,0:T(8,128)(2,1)} %shard_map.101), channel_id=1, replica_groups=mesh['zh'=2,'x'=4,'core'=2,'y'=8,'z'=8] {'y','z'}, dimensions={0} | all-to-all | bytes 262144 | tf_op jit(solution)/shard_map/all_to_all | solution.py:29
  113.3 2.1 %shard_map.102 = (f32[128,128]{1,0:T(8,128)S(1)}, f32[8,24,128]{2,1,0:T(8,128)}) custom-call(bf16[512,128]{1,0:T(8,128)(2,1)S(1)} %bitcast.15, bf16[128,128]{1,0:T(8,128)(2,1)} %conv.5, bf16[256,128]{1,0:T(8,128)(2,1)} %dt_weight.1, f32[1,128]{1,0:T(1,128)} %bitcast.28, f32[16,128]{1,0:T(8,128)} %bitcast.18), custom_call_target="tpu_custom_call" | custom-call | tf_op jit(solution)/shard_map/pallas_call | solution.py:265
  115.3 4.5 %all-to-all-start.2 = ((f32[8,24,128]{2,1,0:T(8,128)}), f32[8,24,128]{2,1,0:T(8,128)S(1)}, u32[]{:S(2)}, u32[]{:S(2)}) async-start(f32[8,24,128]{2,1,0:T(8,128)} %get-tuple-element.14), calls=%async_computation.2 | async-start | bytes 196608 | tf_op jit(solution)/shard_map/all_to_all | solution.py:29
  119.8 3.7 %all-to-all-done.2.gathered = f32[8,24,128]{2,1,0:T(8,128)S(1)} async-done(((f32[8,24,128]{2,1,0:T(8,128)}), f32[8,24,128]{2,1,0:T(8,128)S(1)}, u32[]{:S(2)}, u32[]{:S(2)}) %all-to-all-start.2) | async-done | bytes 98336 | tf_op jit(solution)/shard_map/all_to_all | solution.py:29
  123.6 0.1 shard_map.104
  123.7 11.7 %collective-permute-start = (f32[24,128]{1,0:T(8,128)S(1)}, f32[24,128]{1,0:T(8,128)S(1)}, u32[]{:S(2)}, u32[]{:S(2)}) collective-permute-start(f32[24,128]{1,0:T(8,128)S(1)} %get-tuple-element.15), channel_id=1, source_target_pairs={{0,512},{1,513},{2,514},{3,515},{4,516},{5,517},{6,518},{7,519},{8... | collective-permute-start | bytes 36872 | tf_op jit(solution)/shard_map/ppermute | solution.py:275
  135.3 1.6 shard_map.103
  136.9 0.0 collective-permute-done.6.swapped
  137.0 0.0 copy-start.1
  137.0 0.0 copy-start.2
  137.0 1.7 shard_map.105.gate_pre
  138.7 0.5 shard_map.106
  139.2 14.1 %all_to_all.26.gated = bf16[8,128,128]{2,1,0:T(8,128)(2,1)S(1)} all-to-all(bf16[8,128,128]{2,1,0:T(8,128)(2,1)S(1)} %shard_map.106), channel_id=1, replica_groups=mesh['zh'=2,'x'=4,'core'=2,'y'=8,'z'=8] {'y'}, dimensions={0} | all-to-all | bytes 524288 | tf_op jit(solution)/shard_map/all_to_all | solution.py:29
  153.3 0.5 shard_map.107
  153.9 19.5 %all_to_all.27.shares = bf16[64,8,128]{2,1,0:T(8,128)(2,1)S(1)} all-to-all(bf16[64,8,128]{2,1,0:T(8,128)(2,1)S(1)} %shard_map.107), channel_id=1, replica_groups=mesh['zh'=2,'x'=4,'core'=2,'y'=8,'z'=8] {'y','z'}, dimensions={0} | all-to-all | bytes 262144 | tf_op jit(solution)/shard_map/all_to_all | solution.py:29
  173.4 0.7 shard_map.108
  (11 shorter events, 0.1 us)
Async XLA Ops:
  0.0 40.9 %copy-start.3 = (bf16[256,128]{1,0:T(8,128)(2,1)S(1)}, bf16[256,128]{1,0:T(8,128)(2,1)}, u32[]{:S(2)}) copy-start(bf16[256,128]{1,0:T(8,128)(2,1)} %param.13) | copy-start | bytes 196612
  0.0 10.4 %collective-permute-start.1 = (bf16[256,128]{1,0:T(8,128)(2,1)}, bf16[256,128]{1,0:T(8,128)(2,1)S(1)}, u32[]{:S(2)}, u32[]{:S(2)}) collective-permute-start(bf16[256,128]{1,0:T(8,128)(2,1)} %param.19), channel_id=1, source_target_pairs={{0,0},{8,128},{16,256},{24,384},{32,512},{40,640},{48,768},{56,896... | collective-permute-start | bytes 196616 | tf_op jit(solution)/shard_map/ppermute | solution.py:240
  11.3 38.2 %collective-permute-start.2 = (bf16[512,128]{1,0:T(8,128)(2,1)S(1)}, bf16[512,128]{1,0:T(8,128)(2,1)S(1)}, u32[]{:S(2)}, u32[]{:S(2)}) collective-permute-start(bf16[512,128]{1,0:T(8,128)(2,1)S(1)} %pad_maximum_fusion.1), channel_id=1, source_target_pairs={{0,512},{512,0},{1,513},{513,1},{2,514},{514,2},{3,515},{515,3},{4... | collective-permute-start | bytes 393224 | tf_op jit(solution)/shard_map/ppermute | solution.py:242
  49.4 26.5 %collective-permute-start.5 = (bf16[1024,128]{1,0:T(8,128)(2,1)S(1)}, bf16[1024,128]{1,0:T(8,128)(2,1)S(1)}, u32[]{:S(2)}, u32[]{:S(2)}) collective-permute-start(bf16[1024,128]{1,0:T(8,128)(2,1)S(1)} %constant_dynamic-update-slice_fusion), channel_id=1, source_target_pairs={{0,384},{128,0},{256,128},{384,256},{1,385},{129,1},{257,129},{385... | collective-permute-start | bytes 786440 | tf_op jit(solution)/shard_map/ppermute | solution.py:258
  54.7 21.2 %collective-permute-start.4 = (bf16[1024,128]{1,0:T(8,128)(2,1)S(1)}, bf16[1024,128]{1,0:T(8,128)(2,1)S(1)}, u32[]{:S(2)}, u32[]{:S(2)}) collective-permute-start(bf16[1024,128]{1,0:T(8,128)(2,1)S(1)} %constant_dynamic-update-slice_fusion), channel_id=1, source_target_pairs={{0,256},{128,384},{256,0},{384,128},{1,257},{129,385},{257,1},{385... | collective-permute-start | bytes 786440 | tf_op jit(solution)/shard_map/ppermute | solution.py:258
  56.9 19.0 %collective-permute-start.3 = (bf16[1024,128]{1,0:T(8,128)(2,1)S(1)}, bf16[1024,128]{1,0:T(8,128)(2,1)S(1)}, u32[]{:S(2)}, u32[]{:S(2)}) collective-permute-start(bf16[1024,128]{1,0:T(8,128)(2,1)S(1)} %constant_dynamic-update-slice_fusion), channel_id=1, source_target_pairs={{0,128},{128,256},{256,384},{384,0},{1,129},{129,257},{257,385},{3... | collective-permute-start | bytes 786440 | tf_op jit(solution)/shard_map/ppermute | solution.py:258
  62.9 28.8 %all-to-all-start = ((bf16[64,8,128]{2,1,0:T(8,128)(2,1)}), bf16[64,8,128]{2,1,0:T(8,128)(2,1)S(1)}, u32[]{:S(2)}, u32[]{:S(2)}) async-start(bf16[64,8,128]{2,1,0:T(8,128)(2,1)} %shard_map.100), calls=%async_computation | async-start | bytes 262144 | tf_op jit(solution)/shard_map/all_to_all | solution.py:29
  76.1 60.9 %collective-permute-start.6 = (bf16[4,1024,128]{2,1,0:T(8,128)(2,1)S(1)}, bf16[4,1024,128]{2,1,0:T(8,128)(2,1)S(1)}, u32[]{:S(2)}, u32[]{:S(2)}) collective-permute-start(bf16[4,1024,128]{2,1,0:T(8,128)(2,1)S(1)} %pad_maximum_fusion.kept), channel_id=1, source_target_pairs={{0,64},{64,0},{1,65},{65,1},{2,66},{66,2},{3,67},{67,3},{4,68},{68... | collective-permute-start | bytes 3145736 | tf_op jit(solution)/shard_map/ppermute | solution.py:260
  115.3 8.2 %all-to-all-start.2 = ((f32[8,24,128]{2,1,0:T(8,128)}), f32[8,24,128]{2,1,0:T(8,128)S(1)}, u32[]{:S(2)}, u32[]{:S(2)}) async-start(f32[8,24,128]{2,1,0:T(8,128)} %get-tuple-element.14), calls=%async_computation.2 | async-start | bytes 196608 | tf_op jit(solution)/shard_map/all_to_all | solution.py:29
  119.8 3.7 %copy-start = (f32[128,16]{0,1:T(8,128)S(1)}, f32[128,16]{0,1:T(8,128)}, u32[]{:S(2)}) copy-start(f32[128,16]{0,1:T(8,128)} %param.17) | copy-start | bytes 24580
  123.7 15.0 %collective-permute-start = (f32[24,128]{1,0:T(8,128)S(1)}, f32[24,128]{1,0:T(8,128)S(1)}, u32[]{:S(2)}, u32[]{:S(2)}) collective-permute-start(f32[24,128]{1,0:T(8,128)S(1)} %get-tuple-element.15), channel_id=1, source_target_pairs={{0,512},{1,513},{2,514},{3,515},{4,516},{5,517},{6,518},{7,519},{8... | collective-permute-start | bytes 36872 | tf_op jit(solution)/shard_map/ppermute | solution.py:275
  137.0 1.7 copy-start.1
  137.0 1.7 copy-start.2
